TPU v7x, 32 devices: a whole 2x2x4 slice. The times are simulated.
32 devices in a mesh: ctx: 16 (over z, y, core), tp: 2 (over x).
Axes of the slice: x: 2, y: 2, z: 4, core: 2. Of those that a mesh axis runs over, the one named last changes fastest.
Arguments:
- key_value: bfloat16 [4096, 4, 256], P('ctx', 'tp'), may hold values from -6 to 6
- queries: bfloat16 [4096, 32, 128], P('ctx', 'tp')
- doc_lengths: int32 [8], replicated, may hold values from 1 to 1024, 4096 in all
Outputs:
- attended: bfloat16 [4096, 32, 128], P('ctx', 'tp')
Inputs may be any that keep to these rules, and one draw needn't show every extreme that they name: `doc_lengths`: the lengths sum to 4096 and the longest is exactly 1024.
All inputs are finite; a program needn't handle non-finite values.
Results may differ from a plain program's by a relative error of at most 0.017.
The roundings to bfloat16 on the way count: a program that leaves them out, or rounds other values in their place, can miss the bound.
Values may be sent and summed in bfloat16 or wider, within the bound.
No kernel may reach another device: no remote copies, remote signals or barrier semaphores. Data moves between devices by JAX's collectives and lax.ppermute only.
A program may use at most 64 MiB of HBM per device.

v0:
```python
import math

import jax
import jax.numpy as jnp
from jax import lax
from jax.sharding import PartitionSpec as P

WINDOW = 8


ROPE_BASE = 500000.0
MASKED = -1e30


def from_behind(value, axis, steps):
    count = lax.axis_size(axis)
    leading, last = (max(0, -steps), min(count, count - steps))
    return lax.ppermute(value, axis, [(source, source + steps) for source in range(leading, last)])


def rotate(vectors, positions):
    width = vectors.shape[-1]
    half = width // 2
    inverse_freq = ROPE_BASE ** (-(jnp.arange(half, dtype=jnp.float32) * 2.0 / width))
    angles = positions.astype(jnp.float32)[..., None] * inverse_freq
    cosine = jnp.cos(angles)[..., None, :]
    sine_part = jnp.sin(angles)[..., None, :]
    front_half = vectors[..., :half]
    back_half = vectors[..., half:]
    return jnp.concatenate(
        [front_half * cosine - back_half * sine_part, back_half * cosine + front_half * sine_part],
        axis=-1,
    )


def shards(key_value, queries, doc_lengths):
    rows = key_value.shape[0]
    kv_heads = key_value.shape[1]
    pair_width = key_value.shape[2]
    head_size = queries.shape[-1]
    q_heads = queries.shape[1]
    group_size = q_heads // kv_heads
    half_rows = rows // 2
    score_scale = 1.0 / math.sqrt(head_size)
    devices = lax.axis_size("ctx")
    my_index = lax.axis_index("ctx")
    doc_ends = jnp.cumsum(doc_lengths)
    offsets = jnp.arange(half_rows, dtype=jnp.int32)

    def locate(block_ids):
        place = block_ids[:, None] * half_rows + offsets[None, :]
        document = jnp.sum((place[:, :, None] >= doc_ends[None, None, :]).astype(jnp.int32), axis=2)
        return (place, document)

    own_blocks = jnp.stack([my_index, 2 * devices - 1 - my_index])
    own_place, own_doc = locate(own_blocks)
    pairs = key_value.reshape(2, half_rows, kv_heads, pair_width)
    rotated_kv = jnp.concatenate(
        [
            rotate(pairs[..., :head_size].astype(jnp.float32), own_place),
            pairs[..., head_size:].astype(jnp.float32),
        ],
        axis=-1,
    ).astype(jnp.bfloat16)
    rotated = (
        rotate(queries.reshape(2, half_rows, q_heads, head_size).astype(jnp.float32), own_place)
        .astype(jnp.bfloat16)
        .reshape(2, half_rows, kv_heads, group_size, head_size)
    )

    def attend(carry, key_block, key_blocks):
        running_max, running_sum, running_out = carry
        key_place, key_doc = locate(key_blocks)
        allowed = (
            (key_doc[:, None, :] == own_doc[:, :, None])
            & (key_place[:, None, :] <= own_place[:, :, None])
            & (key_blocks >= 0)[:, None, None]
        )
        scores = (
            jnp.einsum(
                "sthgc,snhc->sthgn",
                rotated,
                key_block[..., :head_size],
                preferred_element_type=jnp.float32,
            )
            * score_scale
        )
        visible = allowed[:, :, None, None, :]
        block_max = jnp.max(jnp.where(visible, scores, MASKED), axis=-1)
        new_max = jnp.maximum(running_max, block_max)
        weights = jnp.where(visible, jnp.exp(scores - new_max[..., None]), 0.0)
        factor = jnp.exp(running_max - new_max)
        new_sum = running_sum * factor + jnp.sum(weights, axis=-1)
        rounded_weights = weights.astype(jnp.bfloat16)
        new_out = running_out * factor[..., None] + jnp.einsum(
            "sthgn,snhc->sthgc",
            rounded_weights,
            key_block[..., head_size:],
            preferred_element_type=jnp.float32,
        )
        return (new_max, new_sum, new_out)

    initial = (
        jnp.full((2, half_rows, kv_heads, group_size), MASKED, jnp.float32),
        jnp.zeros((2, half_rows, kv_heads, group_size), jnp.float32),
        jnp.zeros((2, half_rows, kv_heads, group_size, head_size), jnp.float32),
    )
    carry = attend(initial, rotated_kv, own_blocks)
    at_fold = my_index == devices - 1
    stream = rotated_kv
    for step in range(1, WINDOW + 1):
        rising = from_behind(stream[0], "ctx", 1)
        falling = from_behind(stream[1], "ctx", -1)
        falling = jnp.where(at_fold, stream[0], falling)
        stream = jnp.stack([rising, falling])
        carry = attend(carry, stream, own_blocks - step)
    result = carry[2] / carry[1][..., None]
    return result.reshape(rows, q_heads, head_size).astype(jnp.bfloat16)


def solution(mesh):
    in_specs = (P("ctx", "tp", None), P("ctx", "tp", None), P())
    out_specs = P("ctx", "tp", None)
    return jax.shard_map(shards, mesh=mesh, in_specs=in_specs, out_specs=out_specs, check_vma=False)
```

profile of v0, /device:TPU:26, one launch (start us, length us, event | category | flops | bytes accessed | tf_op | source)
XLA Modules:
  0.0 100.1 jit_solution(17814682855542177639)
XLA Ops:
  0.0 0.6 add_compare_fusion
  0.7 0.6 add_multiply_fusion.1
  1.4 1.0 copy.30
  3.3 0.7 slice_bitcast_fusion
  4.0 2.7 %collective-permute-start.1 = (bf16[128,2,256]{2,0,1:T(8,128)(2,1)}, bf16[128,2,256]{2,0,1:T(8,128)(2,1)}, u32[]{:S(2)}, u32[]{:S(2)}) collective-permute-start(bf16[128,2,256]{2,0,1:T(8,128)(2,1)} %get-tuple-element.39), channel_id=1, source_target_pairs={{2,0},{4,2},{6,4},{8,6},{10,8},{12,10},{14,12},{16,14},{18,16},{20... | collective-permute-start | bytes 393224 | tf_op jit(solution)/shard_map/ppermute | solution.py:18
  6.8 1.9 %collective-permute-start = (bf16[128,2,256]{2,0,1:T(8,128)(2,1)}, bf16[128,2,256]{2,0,1:T(8,128)(2,1)}, u32[]{:S(2)}, u32[]{:S(2)}) collective-permute-start(bf16[128,2,256]{2,0,1:T(8,128)(2,1)} %get-tuple-element.40), channel_id=1, source_target_pairs={{0,2},{2,4},{4,6},{6,8},{8,10},{10,12},{12,14},{14,16},{16,18},{18... | collective-permute-start | bytes 393224 | tf_op jit(solution)/shard_map/ppermute | solution.py:18
  8.7 0.6 broadcast_compare_fusion
  9.3 1.8 %fusion.208 = (f32[2,128,16,64]{3,2,1,0:T(8,128)S(1)}, f32[2,128,16,64]{3,2,1,0:T(8,128)}) fusion(bf16[2,128,16,128]{3,2,1,0:T(8,128)(2,1)S(1)} %bitcast.330), kind=kLoop, calls=%fused_computation.311 | loop fusion | bytes 4194304 | tf_op jit(solution)/shard_map/slice | solution.py:28
  11.1 0.8 reduce-window.8
  11.9 0.7 iota_add_fusion
  12.6 0.8 iota_add_fusion.2
  13.4 0.8 iota_add_fusion.4
  14.1 0.7 iota_add_fusion.6
  14.9 3.0 %subtract_convert_fusion = (bf16[2,128,16,64]{3,1,2,0:T(8,128)(2,1)S(1)}, bf16[2,128,16,64]{3,1,2,0:T(8,128)(2,1)S(1)}) fusion(f32[2,128,16,64]{3,2,1,0:T(8,128)} %get-tuple-element.36, f32[2,128,16,64]{3,2,1,0:T(8,128)S(1)} %get-tuple-element.35, f32[2,128,64]{2,1,0:T(8,128)} %copy-done.2, f32[2,128,64]{2,1,0:T(8,128)} %copy-done.1), kind=kLoop, calls=%fused_computation.65 | loop fusion | flops 2097152 | bytes 3276800 | tf_op jit(solution)/shard_map/convert.4
  18.8 0.6 and_and_fusion.8
  20.2 0.9 broadcast_select_fusion.6
  21.2 4.5 %collective-permute-start.3 = (bf16[128,2,256]{2,0,1:T(8,128)(2,1)S(1)}, bf16[128,2,256]{2,0,1:T(8,128)(2,1)S(1)}, u32[]{:S(2)}, u32[]{:S(2)}) collective-permute-start(bf16[128,2,256]{2,0,1:T(8,128)(2,1)S(1)} %broadcast_select_fusion.6), channel_id=1, source_target_pairs={{2,0},{4,2},{6,4},{8,6},{10,8},{12,10},{14,12},{16,14},{18,16},{20... | collective-permute-start | bytes 393224 | tf_op jit(solution)/shard_map/ppermute | solution.py:18
  25.7 1.3 %fusion.30 = (f32[2,128,2,8]{1,3,2,0:T(8,128)S(1)}, f32[2,2,128,128,8]{3,2,4,1,0:T(8,128)S(1)}) fusion(pred[2,128,128]{1,2,0:T(8,128)(4,1)S(1)} %get-tuple-element.51, bf16[2,128,2,8,128]{4,1,3,2,0:T(8,128)(2,1)S(1)} %pad_maximum_fusion, bf16[1,128,2,256]{3,1,2,0:T(8,128)(2,1)} %bitcast.16, bf16[1,128,2,256]{3,1,2,0:T(8,128)(2,1)S(1)} %bitcast.333), kind=kOutput, calls=%fused_computation.54 | convolution fusion | flops 136048640 | bytes 3457024 | tf_op jit(solution)/shard_map/sthgc,snhc->sthgn/dot_general | solution.py:80
  27.0 1.9 %collective-permute-start.2 = (bf16[128,2,256]{2,0,1:T(8,128)(2,1)}, bf16[128,2,256]{2,0,1:T(8,128)(2,1)S(1)}, u32[]{:S(2)}, u32[]{:S(2)}) collective-permute-start(bf16[128,2,256]{2,0,1:T(8,128)(2,1)} %collective-permute-done), channel_id=1, source_target_pairs={{0,2},{2,4},{4,6},{6,8},{8,10},{10,12},{12,14},{14,16},{16,18},{18... | collective-permute-start | bytes 393224 | tf_op jit(solution)/shard_map/ppermute | solution.py:18
  29.0 4.5 %collective-permute-start.5 = (bf16[128,2,256]{2,0,1:T(8,128)(2,1)S(1)}, bf16[128,2,256]{2,0,1:T(8,128)(2,1)S(1)}, u32[]{:S(2)}, u32[]{:S(2)}) collective-permute-start(bf16[128,2,256]{2,0,1:T(8,128)(2,1)S(1)} %broadcast_select_fusion.5), channel_id=1, source_target_pairs={{2,0},{4,2},{6,4},{8,6},{10,8},{12,10},{14,12},{16,14},{18,16},{20... | collective-permute-start | bytes 393224 | tf_op jit(solution)/shard_map/ppermute | solution.py:18
  33.6 0.9 collective-permute-done.2
  35.0 1.9 %collective-permute-start.4 = (bf16[128,2,256]{2,0,1:T(8,128)(2,1)S(1)}, bf16[128,2,256]{2,0,1:T(8,128)(2,1)S(1)}, u32[]{:S(2)}, u32[]{:S(2)}) collective-permute-start(bf16[128,2,256]{2,0,1:T(8,128)(2,1)S(1)} %collective-permute-done.2), channel_id=1, source_target_pairs={{0,2},{2,4},{4,6},{6,8},{8,10},{10,12},{12,14},{14,16},{16,18},{18... | collective-permute-start | bytes 393224 | tf_op jit(solution)/shard_map/ppermute | solution.py:18
  36.9 4.5 %collective-permute-start.7 = (bf16[128,2,256]{2,0,1:T(8,128)(2,1)S(1)}, bf16[128,2,256]{2,0,1:T(8,128)(2,1)S(1)}, u32[]{:S(2)}, u32[]{:S(2)}) collective-permute-start(bf16[128,2,256]{2,0,1:T(8,128)(2,1)S(1)} %broadcast_select_fusion.4), channel_id=1, source_target_pairs={{2,0},{4,2},{6,4},{8,6},{10,8},{12,10},{14,12},{16,14},{18,16},{20... | collective-permute-start | bytes 393224 | tf_op jit(solution)/shard_map/ppermute | solution.py:18
  41.5 0.8 collective-permute-done.4
  42.7 1.9 %collective-permute-start.6 = (bf16[128,2,256]{2,0,1:T(8,128)(2,1)S(1)}, bf16[128,2,256]{2,0,1:T(8,128)(2,1)S(1)}, u32[]{:S(2)}, u32[]{:S(2)}) collective-permute-start(bf16[128,2,256]{2,0,1:T(8,128)(2,1)S(1)} %collective-permute-done.4), channel_id=1, source_target_pairs={{0,2},{2,4},{4,6},{6,8},{8,10},{10,12},{12,14},{14,16},{16,18},{18... | collective-permute-start | bytes 393224 | tf_op jit(solution)/shard_map/ppermute | solution.py:18
  44.7 4.5 %collective-permute-start.9 = (bf16[128,2,256]{2,0,1:T(8,128)(2,1)S(1)}, bf16[128,2,256]{2,0,1:T(8,128)(2,1)S(1)}, u32[]{:S(2)}, u32[]{:S(2)}) collective-permute-start(bf16[128,2,256]{2,0,1:T(8,128)(2,1)S(1)} %broadcast_select_fusion.3), channel_id=1, source_target_pairs={{2,0},{4,2},{6,4},{8,6},{10,8},{12,10},{14,12},{16,14},{18,16},{20... | collective-permute-start | bytes 393224 | tf_op jit(solution)/shard_map/ppermute | solution.py:18
  49.2 0.8 collective-permute-done.6
  50.5 1.9 %collective-permute-start.8 = (bf16[128,2,256]{2,0,1:T(8,128)(2,1)S(1)}, bf16[128,2,256]{2,0,1:T(8,128)(2,1)S(1)}, u32[]{:S(2)}, u32[]{:S(2)}) collective-permute-start(bf16[128,2,256]{2,0,1:T(8,128)(2,1)S(1)} %collective-permute-done.6), channel_id=1, source_target_pairs={{0,2},{2,4},{4,6},{6,8},{8,10},{10,12},{12,14},{14,16},{16,18},{18... | collective-permute-start | bytes 393224 | tf_op jit(solution)/shard_map/ppermute | solution.py:18
  52.4 4.5 %collective-permute-start.11 = (bf16[128,2,256]{2,0,1:T(8,128)(2,1)S(1)}, bf16[128,2,256]{2,0,1:T(8,128)(2,1)S(1)}, u32[]{:S(2)}, u32[]{:S(2)}) collective-permute-start(bf16[128,2,256]{2,0,1:T(8,128)(2,1)S(1)} %broadcast_select_fusion.2), channel_id=1, source_target_pairs={{2,0},{4,2},{6,4},{8,6},{10,8},{12,10},{14,12},{16,14},{18,16},{20... | collective-permute-start | bytes 393224 | tf_op jit(solution)/shard_map/ppermute | solution.py:18
  57.0 0.8 collective-permute-done.8
  58.2 1.9 %collective-permute-start.10 = (bf16[128,2,256]{2,0,1:T(8,128)(2,1)S(1)}, bf16[128,2,256]{2,0,1:T(8,128)(2,1)S(1)}, u32[]{:S(2)}, u32[]{:S(2)}) collective-permute-start(bf16[128,2,256]{2,0,1:T(8,128)(2,1)S(1)} %collective-permute-done.8), channel_id=1, source_target_pairs={{0,2},{2,4},{4,6},{6,8},{8,10},{10,12},{12,14},{14,16},{16,18},{18... | collective-permute-start | bytes 393224 | tf_op jit(solution)/shard_map/ppermute | solution.py:18
  60.2 4.5 %collective-permute-start.13 = (bf16[128,2,256]{2,0,1:T(8,128)(2,1)S(1)}, bf16[128,2,256]{2,0,1:T(8,128)(2,1)S(1)}, u32[]{:S(2)}, u32[]{:S(2)}) collective-permute-start(bf16[128,2,256]{2,0,1:T(8,128)(2,1)S(1)} %broadcast_select_fusion.1), channel_id=1, source_target_pairs={{2,0},{4,2},{6,4},{8,6},{10,8},{12,10},{14,12},{16,14},{18,16},{20... | collective-permute-start | bytes 393224 | tf_op jit(solution)/shard_map/ppermute | solution.py:18
  64.7 0.8 collective-permute-done.10
  66.0 1.9 %collective-permute-start.12 = (bf16[128,2,256]{2,0,1:T(8,128)(2,1)S(1)}, bf16[128,2,256]{2,0,1:T(8,128)(2,1)S(1)}, u32[]{:S(2)}, u32[]{:S(2)}) collective-permute-start(bf16[128,2,256]{2,0,1:T(8,128)(2,1)S(1)} %collective-permute-done.10), channel_id=1, source_target_pairs={{0,2},{2,4},{4,6},{6,8},{8,10},{10,12},{12,14},{14,16},{16,18},{18... | collective-permute-start | bytes 393224 | tf_op jit(solution)/shard_map/ppermute | solution.py:18
  68.0 4.5 %collective-permute-start.15 = (bf16[128,2,256]{2,0,1:T(8,128)(2,1)S(1)}, bf16[128,2,256]{2,0,1:T(8,128)(2,1)S(1)}, u32[]{:S(2)}, u32[]{:S(2)}) collective-permute-start(bf16[128,2,256]{2,0,1:T(8,128)(2,1)S(1)} %broadcast_select_fusion), channel_id=1, source_target_pairs={{2,0},{4,2},{6,4},{8,6},{10,8},{12,10},{14,12},{16,14},{18,16},{20... | collective-permute-start | bytes 393224 | tf_op jit(solution)/shard_map/ppermute | solution.py:18
  72.5 0.8 collective-permute-done.12
  73.7 2.1 %collective-permute-start.14 = (bf16[128,2,256]{2,0,1:T(8,128)(2,1)S(1)}, bf16[128,2,256]{2,0,1:T(8,128)(2,1)S(1)}, u32[]{:S(2)}, u32[]{:S(2)}) collective-permute-start(bf16[128,2,256]{2,0,1:T(8,128)(2,1)S(1)} %collective-permute-done.12), channel_id=1, source_target_pairs={{0,2},{2,4},{4,6},{6,8},{8,10},{10,12},{12,14},{14,16},{16,18},{18... | collective-permute-start | bytes 393224 | tf_op jit(solution)/shard_map/ppermute | solution.py:18
  75.9 5.0 %collective-permute-done.14 = bf16[128,2,256]{2,0,1:T(8,128)(2,1)S(1)} collective-permute-done((bf16[128,2,256]{2,0,1:T(8,128)(2,1)S(1)}, bf16[128,2,256]{2,0,1:T(8,128)(2,1)S(1)}, u32[]{:S(2)}, u32[]{:S(2)}) %collective-permute-start.14) | collective-permute-done | bytes 131104 | tf_op jit(solution)/shard_map/ppermute | solution.py:18
  81.9 0.7 fusion.70
  83.1 0.7 fusion.56
  84.2 0.7 fusion.58
  85.4 0.7 fusion.60
  86.5 0.7 fusion.62
  87.7 0.7 fusion.64
  88.8 0.7 fusion.66
  90.0 1.5 %fusion.68 = f32[2,2,128,128,8]{2,3,4,1,0:T(8,128)S(1)} fusion(f32[2,2,128,128,8]{3,2,4,1,0:T(8,128)S(1)} %get-tuple-element.90, f32[2,128,2,8]{1,3,2,0:T(8,128)S(1)} %get-tuple-element.30, pred[2,128,128]{1,2,0:T(8,128)(4,1)S(1)} %get-tuple-element.51, bf16[1,128,2,256]{3,1,2,0:T(8,128)(2,1)S(1)} %bitcast.334, bf16[1,128,2,256]{3,1,2,0:T(8,128)(2,1)} %bitcast.16), kind=kOutput, calls=%fused_computation.90 | convolution fusion | flops 136577024 | bytes 4505600 | tf_op jit(solution)/shard_map/sthgn,snhc->sthgc/dot_general | solution.py:95
  92.0 6.3 %fusion.1 = bf16[2,128,2,8,128]{4,1,3,2,0:T(8,128)(2,1)S(1)} fusion(f32[2,2,128,128,8]{2,3,4,1,0:T(8,128)S(1)} %fusion.56, f32[2,2,128,128,8]{2,3,4,1,0:T(8,128)S(1)} %fusion.58, f32[2,2,128,128,8]{2,3,4,1,0:T(8,128)S(1)} %fusion.60, f32[2,2,128,128,8]{2,3,4,1,0:T(8,128)S(1)} %fusion.62, f32[2,2,128,128,8]{2,3,4,1,0:T(8,128)S(1)} %fusion.64, ...), kind=kOutput, calls=%fused_computation.2 | convolution fusion | flops 146538496 | bytes 20398080 | tf_op jit(solution)/shard_map/sthgn,snhc->sthgc/dot_general | solution.py:95
  98.4 1.6 %copy.44 = bf16[2,128,2,8,128]{4,3,2,1,0:T(8,128)(2,1)} copy(bf16[2,128,2,8,128]{4,1,3,2,0:T(8,128)(2,1)S(1)} %fusion.1) | data formatting | bytes 2097152 | tf_op jit(solution)/shard_map/convert_element_type | solution.py:118
  (71 shorter events, 10.3 us)
Async XLA Ops:
  0.0 9.3 %copy-start = (bf16[256,16,128]{2,1,0:T(8,128)(2,1)S(1)}, bf16[256,16,128]{2,1,0:T(8,128)(2,1)}, u32[]{:S(2)}) copy-start(bf16[256,16,128]{2,1,0:T(8,128)(2,1)} %param.4) | copy-start | bytes 3145732
  3.0 6.4 %copy-start.1 = (f32[2,128,64]{2,1,0:T(8,128)}, f32[2,128,64]{2,1,0:T(8,128)S(1)}, u32[]{:S(2)}) copy-start(f32[2,128,64]{2,1,0:T(8,128)S(1)} %get-tuple-element.54) | copy-start | bytes 196612
  3.0 6.3 %copy-start.2 = (f32[2,128,64]{2,1,0:T(8,128)}, f32[2,128,64]{2,1,0:T(8,128)S(1)}, u32[]{:S(2)}) copy-start(f32[2,128,64]{2,1,0:T(8,128)S(1)} %get-tuple-element.55) | copy-start | bytes 196612
  3.1 6.2 %copy-start.3 = (bf16[2,128,2,64]{3,1,2,0:T(8,128)(2,1)}, bf16[2,128,2,64]{3,1,2,0:T(8,128)(2,1)S(1)}, u32[]{:S(2)}) copy-start(bf16[2,128,2,64]{3,1,2,0:T(8,128)(2,1)S(1)} %get-tuple-element.37) | copy-start | bytes 196612
  3.1 6.2 %copy-start.5 = (bf16[2,128,2,64]{3,1,2,0:T(8,128)(2,1)}, bf16[2,128,2,64]{3,1,2,0:T(8,128)(2,1)S(1)}, u32[]{:S(2)}) copy-start(bf16[2,128,2,64]{3,1,2,0:T(8,128)(2,1)S(1)} %get-tuple-element.38) | copy-start | bytes 196612
  4.0 16.2 %collective-permute-start.1 = (bf16[128,2,256]{2,0,1:T(8,128)(2,1)}, bf16[128,2,256]{2,0,1:T(8,128)(2,1)}, u32[]{:S(2)}, u32[]{:S(2)}) collective-permute-start(bf16[128,2,256]{2,0,1:T(8,128)(2,1)} %get-tuple-element.39), channel_id=1, source_target_pairs={{2,0},{4,2},{6,4},{8,6},{10,8},{12,10},{14,12},{16,14},{18,16},{20... | collective-permute-start | bytes 393224 | tf_op jit(solution)/shard_map/ppermute | solution.py:18
  6.8 18.9 %collective-permute-start = (bf16[128,2,256]{2,0,1:T(8,128)(2,1)}, bf16[128,2,256]{2,0,1:T(8,128)(2,1)}, u32[]{:S(2)}, u32[]{:S(2)}) collective-permute-start(bf16[128,2,256]{2,0,1:T(8,128)(2,1)} %get-tuple-element.40), channel_id=1, source_target_pairs={{0,2},{2,4},{4,6},{6,8},{8,10},{10,12},{12,14},{14,16},{16,18},{18... | collective-permute-start | bytes 393224 | tf_op jit(solution)/shard_map/ppermute | solution.py:18
  17.9 0.8 copy-start.7
  17.9 0.8 copy-start.8
  17.9 0.8 copy-start.9
  17.9 0.8 copy-start.10
  18.0 0.8 copy-start.11
  18.0 1.4 %copy-start.4 = (bf16[2,128,2,64]{3,1,2,0:T(8,128)(2,1)S(1)}, bf16[2,128,2,64]{3,1,2,0:T(8,128)(2,1)}, u32[]{:S(2)}) copy-start(bf16[2,128,2,64]{3,1,2,0:T(8,128)(2,1)} %copy-done.3) | copy-start | bytes 196612
  18.0 1.4 %copy-start.6 = (bf16[2,128,2,64]{3,1,2,0:T(8,128)(2,1)S(1)}, bf16[2,128,2,64]{3,1,2,0:T(8,128)(2,1)}, u32[]{:S(2)}) copy-start(bf16[2,128,2,64]{3,1,2,0:T(8,128)(2,1)} %copy-done.5) | copy-start | bytes 196612
  18.6 1.3 %copy-start.12 = (pred[2]{0:T(512)(128)(4,1)S(1)}, pred[2]{0:T(512)(128)(4,1)}, u32[]{:S(2)}) copy-start(pred[2]{0:T(512)(128)(4,1)} %get-tuple-element.31) | copy-start | bytes 10
  21.2 7.8 %collective-permute-start.3 = (bf16[128,2,256]{2,0,1:T(8,128)(2,1)S(1)}, bf16[128,2,256]{2,0,1:T(8,128)(2,1)S(1)}, u32[]{:S(2)}, u32[]{:S(2)}) collective-permute-start(bf16[128,2,256]{2,0,1:T(8,128)(2,1)S(1)} %broadcast_select_fusion.6), channel_id=1, source_target_pairs={{2,0},{4,2},{6,4},{8,6},{10,8},{12,10},{14,12},{16,14},{18,16},{20... | collective-permute-start | bytes 393224 | tf_op jit(solution)/shard_map/ppermute | solution.py:18
  27.0 7.4 %collective-permute-start.2 = (bf16[128,2,256]{2,0,1:T(8,128)(2,1)}, bf16[128,2,256]{2,0,1:T(8,128)(2,1)S(1)}, u32[]{:S(2)}, u32[]{:S(2)}) collective-permute-start(bf16[128,2,256]{2,0,1:T(8,128)(2,1)} %collective-permute-done), channel_id=1, source_target_pairs={{0,2},{2,4},{4,6},{6,8},{8,10},{10,12},{12,14},{14,16},{16,18},{18... | collective-permute-start | bytes 393224 | tf_op jit(solution)/shard_map/ppermute | solution.py:18
  29.0 7.9 %collective-permute-start.5 = (bf16[128,2,256]{2,0,1:T(8,128)(2,1)S(1)}, bf16[128,2,256]{2,0,1:T(8,128)(2,1)S(1)}, u32[]{:S(2)}, u32[]{:S(2)}) collective-permute-start(bf16[128,2,256]{2,0,1:T(8,128)(2,1)S(1)} %broadcast_select_fusion.5), channel_id=1, source_target_pairs={{2,0},{4,2},{6,4},{8,6},{10,8},{12,10},{14,12},{16,14},{18,16},{20... | collective-permute-start | bytes 393224 | tf_op jit(solution)/shard_map/ppermute | solution.py:18
  35.0 7.3 %collective-permute-start.4 = (bf16[128,2,256]{2,0,1:T(8,128)(2,1)S(1)}, bf16[128,2,256]{2,0,1:T(8,128)(2,1)S(1)}, u32[]{:S(2)}, u32[]{:S(2)}) collective-permute-start(bf16[128,2,256]{2,0,1:T(8,128)(2,1)S(1)} %collective-permute-done.2), channel_id=1, source_target_pairs={{0,2},{2,4},{4,6},{6,8},{8,10},{10,12},{12,14},{14,16},{16,18},{18... | collective-permute-start | bytes 393224 | tf_op jit(solution)/shard_map/ppermute | solution.py:18
  36.9 7.7 %collective-permute-start.7 = (bf16[128,2,256]{2,0,1:T(8,128)(2,1)S(1)}, bf16[128,2,256]{2,0,1:T(8,128)(2,1)S(1)}, u32[]{:S(2)}, u32[]{:S(2)}) collective-permute-start(bf16[128,2,256]{2,0,1:T(8,128)(2,1)S(1)} %broadcast_select_fusion.4), channel_id=1, source_target_pairs={{2,0},{4,2},{6,4},{8,6},{10,8},{12,10},{14,12},{16,14},{18,16},{20... | collective-permute-start | bytes 393224 | tf_op jit(solution)/shard_map/ppermute | solution.py:18
  42.7 7.3 %collective-permute-start.6 = (bf16[128,2,256]{2,0,1:T(8,128)(2,1)S(1)}, bf16[128,2,256]{2,0,1:T(8,128)(2,1)S(1)}, u32[]{:S(2)}, u32[]{:S(2)}) collective-permute-start(bf16[128,2,256]{2,0,1:T(8,128)(2,1)S(1)} %collective-permute-done.4), channel_id=1, source_target_pairs={{0,2},{2,4},{4,6},{6,8},{8,10},{10,12},{12,14},{14,16},{16,18},{18... | collective-permute-start | bytes 393224 | tf_op jit(solution)/shard_map/ppermute | solution.py:18
  44.7 7.7 %collective-permute-start.9 = (bf16[128,2,256]{2,0,1:T(8,128)(2,1)S(1)}, bf16[128,2,256]{2,0,1:T(8,128)(2,1)S(1)}, u32[]{:S(2)}, u32[]{:S(2)}) collective-permute-start(bf16[128,2,256]{2,0,1:T(8,128)(2,1)S(1)} %broadcast_select_fusion.3), channel_id=1, source_target_pairs={{2,0},{4,2},{6,4},{8,6},{10,8},{12,10},{14,12},{16,14},{18,16},{20... | collective-permute-start | bytes 393224 | tf_op jit(solution)/shard_map/ppermute | solution.py:18
  50.5 7.3 %collective-permute-start.8 = (bf16[128,2,256]{2,0,1:T(8,128)(2,1)S(1)}, bf16[128,2,256]{2,0,1:T(8,128)(2,1)S(1)}, u32[]{:S(2)}, u32[]{:S(2)}) collective-permute-start(bf16[128,2,256]{2,0,1:T(8,128)(2,1)S(1)} %collective-permute-done.6), channel_id=1, source_target_pairs={{0,2},{2,4},{4,6},{6,8},{8,10},{10,12},{12,14},{14,16},{16,18},{18... | collective-permute-start | bytes 393224 | tf_op jit(solution)/shard_map/ppermute | solution.py:18
  52.4 7.7 %collective-permute-start.11 = (bf16[128,2,256]{2,0,1:T(8,128)(2,1)S(1)}, bf16[128,2,256]{2,0,1:T(8,128)(2,1)S(1)}, u32[]{:S(2)}, u32[]{:S(2)}) collective-permute-start(bf16[128,2,256]{2,0,1:T(8,128)(2,1)S(1)} %broadcast_select_fusion.2), channel_id=1, source_target_pairs={{2,0},{4,2},{6,4},{8,6},{10,8},{12,10},{14,12},{16,14},{18,16},{20... | collective-permute-start | bytes 393224 | tf_op jit(solution)/shard_map/ppermute | solution.py:18
  58.2 7.3 %collective-permute-start.10 = (bf16[128,2,256]{2,0,1:T(8,128)(2,1)S(1)}, bf16[128,2,256]{2,0,1:T(8,128)(2,1)S(1)}, u32[]{:S(2)}, u32[]{:S(2)}) collective-permute-start(bf16[128,2,256]{2,0,1:T(8,128)(2,1)S(1)} %collective-permute-done.8), channel_id=1, source_target_pairs={{0,2},{2,4},{4,6},{6,8},{8,10},{10,12},{12,14},{14,16},{16,18},{18... | collective-permute-start | bytes 393224 | tf_op jit(solution)/shard_map/ppermute | solution.py:18
  60.2 7.7 %collective-permute-start.13 = (bf16[128,2,256]{2,0,1:T(8,128)(2,1)S(1)}, bf16[128,2,256]{2,0,1:T(8,128)(2,1)S(1)}, u32[]{:S(2)}, u32[]{:S(2)}) collective-permute-start(bf16[128,2,256]{2,0,1:T(8,128)(2,1)S(1)} %broadcast_select_fusion.1), channel_id=1, source_target_pairs={{2,0},{4,2},{6,4},{8,6},{10,8},{12,10},{14,12},{16,14},{18,16},{20... | collective-permute-start | bytes 393224 | tf_op jit(solution)/shard_map/ppermute | solution.py:18
  66.0 7.3 %collective-permute-start.12 = (bf16[128,2,256]{2,0,1:T(8,128)(2,1)S(1)}, bf16[128,2,256]{2,0,1:T(8,128)(2,1)S(1)}, u32[]{:S(2)}, u32[]{:S(2)}) collective-permute-start(bf16[128,2,256]{2,0,1:T(8,128)(2,1)S(1)} %collective-permute-done.10), channel_id=1, source_target_pairs={{0,2},{2,4},{4,6},{6,8},{8,10},{10,12},{12,14},{14,16},{16,18},{18... | collective-permute-start | bytes 393224 | tf_op jit(solution)/shard_map/ppermute | solution.py:18
  68.0 7.9 %collective-permute-start.15 = (bf16[128,2,256]{2,0,1:T(8,128)(2,1)S(1)}, bf16[128,2,256]{2,0,1:T(8,128)(2,1)S(1)}, u32[]{:S(2)}, u32[]{:S(2)}) collective-permute-start(bf16[128,2,256]{2,0,1:T(8,128)(2,1)S(1)} %broadcast_select_fusion), channel_id=1, source_target_pairs={{2,0},{4,2},{6,4},{8,6},{10,8},{12,10},{14,12},{16,14},{18,16},{20... | collective-permute-start | bytes 393224 | tf_op jit(solution)/shard_map/ppermute | solution.py:18
  73.7 7.2 %collective-permute-start.14 = (bf16[128,2,256]{2,0,1:T(8,128)(2,1)S(1)}, bf16[128,2,256]{2,0,1:T(8,128)(2,1)S(1)}, u32[]{:S(2)}, u32[]{:S(2)}) collective-permute-start(bf16[128,2,256]{2,0,1:T(8,128)(2,1)S(1)} %collective-permute-done.12), channel_id=1, source_target_pairs={{0,2},{2,4},{4,6},{6,8},{8,10},{10,12},{12,14},{14,16},{16,18},{18... | collective-permute-start | bytes 393224 | tf_op jit(solution)/shard_map/ppermute | solution.py:18
where the time goes:
time: 101 us; the launch traced here: 100 us
  starting transfers between devices  50.1 us (50%)
  matrix products  17.6 us (17%)
  other arithmetic  16.7 us (17%)
  waiting for transfers between devices  9.86 us (10%)
  local copies, waits for them, and re-layouts  5.22 us (5%)
    ppermute x16, starting transfers between devices, from_behind(): lax.ppermute(value, axis, [(source, source + steps) for source in range(l...  50.1 us
    dot_general x9, matrix products, attend(): jnp.einsum('sthgn,snhc->sthgc', rounded_weights, key_block[..., head_size...  12.6 us
    ppermute x16, waiting for transfers between devices, from_behind(): lax.ppermute(value, axis, [(source, source + steps) for source in range(l...  9.86 us
    dot_general x9, matrix products, attend(): jnp.einsum('sthgc,snhc->sthgn', rotated, key_block[..., :head_size], pref...  5.05 us
    reduce_sum x9, other arithmetic, attend(): new_sum = running_sum * factor + jnp.sum(weights, axis=-1)  4.31 us
    another operation x3, other arithmetic  4.02 us
    add x5, other arithmetic, locate(): place = block_ids[:, None] * half_rows + offsets[None, :]  3.01 us
  transfers between devices with their start and end apart: 16, of which 7 were waited for; matrix products, arithmetic and copies ran while one was open for 16% of the time, Pallas kernels for 0%

commit v1 on v0

v1 whole, which is shorter than its diff:
```python
import functools
import math

import jax
import jax.numpy as jnp
import numpy as np
from jax import lax
from jax.experimental import pallas as pl
from jax.experimental.pallas import tpu as pltpu
from jax.sharding import PartitionSpec as P

ROPE_BASE = 500000.0
HIDDEN = -3.0e38
REACH = 4


def chain_device(chunk, chips):
    return 2 * chunk if chunk < chips else 2 * (2 * chips - 1 - chunk) + 1


def along_chain(value, steps):
    count = lax.axis_size("ctx")
    chips = count // 2
    pairs = [
        (chain_device(c, chips), chain_device(c + steps, chips)) for c in range(count - steps)
    ]
    return lax.ppermute(value, "ctx", pairs)


def to_sibling(value):
    count = lax.axis_size("ctx")
    return lax.ppermute(value, "ctx", [(i, i ^ 1) for i in range(count)])


def my_chunks():
    me = lax.axis_index("ctx")
    count = lax.axis_size("ctx")
    core = lax.rem(me, 2)
    chip = lax.div(me, 2)
    low, high = chip, count - 1 - chip
    mine = jnp.where(core == 0, low, high)
    other = jnp.where(core == 0, high, low)
    return core, mine, other


def swap_halves(x):
    return pltpu.roll(x, x.shape[-1] // 2, axis=x.ndim - 1)


def prepare_kernel(half, docs_ref, freq_ref, q_ref, qrot_ref, cos_ref, sin_ref, base_ref, start_ref, work):
    core, mine, other = my_chunks()
    size = 2 * half
    width = freq_ref.shape[-1]
    groups = qrot_ref.shape[1]
    freq = freq_ref[...]
    steps = lax.broadcasted_iota(jnp.int32, (size, width), 0).astype(jnp.float32)
    angle = steps * freq
    cos_ref[...] = jnp.cos(angle)
    sin_ref[...] = jnp.sin(angle)
    row = lax.broadcasted_iota(jnp.int32, (8, width), 0)
    sign = jnp.where(lax.broadcasted_iota(jnp.int32, (1, width), 1) < width // 2, -1.0, 1.0)
    for stream, chunk in enumerate((mine, other)):
        place = ((chunk - row) * size).astype(jnp.float32) * freq
        base_ref[2 * stream] = jnp.cos(place)
        base_ref[2 * stream + 1] = jnp.sin(place)
    docs = docs_ref.shape[0]
    lanes = lax.broadcasted_iota(jnp.int32, (8, half), 1)
    places = [mine * size + lanes, other * size + half + lanes]

    def doc_step(i, carry):
        end, low, high = carry
        end = end + docs_ref[i]
        return (
            end,
            jnp.where(places[0] >= end, end, low),
            jnp.where(places[1] >= end, end, high),
        )

    zero = jnp.zeros((8, half), jnp.int32)
    _, low, high = lax.fori_loop(0, docs, doc_step, (jnp.int32(0), zero, zero))
    start_ref[0] = low
    start_ref[1] = high
    tokens = 16
    heads = q_ref.shape[1]
    per = heads // groups
    for stream in range(2):
        shift = half * stream
        base_cos = base_ref[2 * stream, 0:1, :]
        base_sin = base_ref[2 * stream + 1, 0:1, :]
        c = cos_ref[pl.ds(shift, half), :]
        s = sin_ref[pl.ds(shift, half), :]
        work[0] = (base_cos * c - base_sin * s)[:, None, :]
        work[1] = ((base_sin * c + base_cos * s) * sign)[:, None, :]
        first = jnp.where(core == 0, half * stream, half * (1 - stream))

        def rope_step(i, carry):
            at = i * tokens
            x = q_ref[pl.ds(first + at, tokens)].astype(jnp.float32)
            y = x * work[0, pl.ds(at, tokens)] + swap_halves(x) * work[1, pl.ds(at, tokens)]
            for g in range(groups):
                piece = y[:, g * per:(g + 1) * per, :].reshape(tokens * per, width)
                rows = pl.ds(pl.multiple_of(at * per, tokens * per), tokens * per)
                qrot_ref[stream, g, rows, :] = piece.astype(jnp.bfloat16)
            return carry

        lax.fori_loop(0, half // tokens, rope_step, 0)


def load_keys(chunk_ref, head, first, count, cos_ref, sin_ref, base_ref, stream, step,
              key_at, starts, first_place, query_base, keys, values, at):
    width = cos_ref.shape[-1]
    sign = jnp.where(lax.broadcasted_iota(jnp.int32, (1, width), 1) < width // 2, -1.0, 1.0)
    base_cos = base_ref[2 * stream, step:step + 1, :]
    base_sin = base_ref[2 * stream + 1, step:step + 1, :]
    c = cos_ref[pl.ds(first, count), :]
    s = sin_ref[pl.ds(first, count), :]
    cosine = base_cos * c - base_sin * s
    sine = (base_sin * c + base_cos * s) * sign
    half = starts.shape[-1]
    place = first_place + first + lax.broadcasted_iota(jnp.int32, (count, half), 0)
    query = query_base + lax.broadcasted_iota(jnp.int32, (count, half), 1)
    visible = (place >= starts) & (place <= query)
    hidden = jnp.where(visible, 0.0, HIDDEN).astype(jnp.bfloat16)
    for g in range(chunk_ref.shape[0]):
        k = chunk_ref[g, pl.ds(first, count), :width].astype(jnp.float32)
        keys[g, pl.ds(at, count), :width] = (k * cosine + swap_halves(k) * sine).astype(jnp.bfloat16)
        keys[g, pl.ds(at, count), width:] = hidden
        values[g, pl.ds(at, count), :width] = chunk_ref[g, pl.ds(first, count), width:]


def one_hot_rows(pick, half, per):
    rows = half * per
    token = lax.broadcasted_iota(jnp.int32, (rows, half), 0) // per
    lane = lax.broadcasted_iota(jnp.int32, (rows, half), 1)
    pick[...] = jnp.where(token == lane, 1.0, 0.0).astype(jnp.bfloat16)


def scores_of(q, pick, k):
    return lax.dot_general(
        jnp.concatenate([q, pick], axis=1), k, (((1,), (1,)), ((), ())),
        preferred_element_type=jnp.float32,
    )


def near_kernel(half, factor, qrot_ref, cos_ref, sin_ref, base_ref, start_ref, own0, own1, a0, a1, b0, b1,
                acc_ref, max_ref, keys, values, pick):
    core, mine, other = my_chunks()
    size = 2 * half
    groups, rows, width = qrot_ref.shape[1:]
    per = rows // half
    one_hot_rows(pick, half, per)
    values[:, :, width:] = jnp.ones(values.shape[:2] + (width,), jnp.bfloat16)
    tile = 256
    for stream, chunk, own, own_count, one, two in ((0, mine, own0, half, a0, b0), (1, other, own1, size, a1, b1)):
        starts = start_ref[stream, 0:1, :]
        query_base = chunk * size + half * stream
        at = 0
        for step, ref, count in ((0, own, own_count), (1, one, size), (2, two, size)):
            load_keys(ref, None, 0, count, cos_ref, sin_ref, base_ref, stream, step, None,
                      starts, (chunk - step) * size, query_base, keys, values, at)
            at += count
        for g in range(groups):
            def body(i, carry):
                r = pl.ds(pl.multiple_of(i * tile, tile), tile)
                s = scores_of(qrot_ref[stream, g, r, :], pick[r, :], keys[g, :at, :])
                top = jnp.max(s, axis=1, keepdims=True)
                p = jnp.exp2((s - top) * factor).astype(jnp.bfloat16)
                acc_ref[stream, g, r, :] = jnp.dot(p, values[g, :at, :], preferred_element_type=jnp.float32)
                max_ref[stream, g, r, :] = jnp.broadcast_to(top, (tile, width))
                return carry

            lax.fori_loop(0, rows // tile, body, 0)


def far_kernel(half, factor, qrot_ref, cos_ref, sin_ref, base_ref, start_ref, acc_ref, max_ref, a0, a1, b0, b1,
               out_ref, keys, values, pick):
    core, mine, other = my_chunks()
    size = 2 * half
    groups, rows, width = qrot_ref.shape[1:]
    per = rows // half
    one_hot_rows(pick, half, per)
    values[:, :, width:] = jnp.ones(values.shape[:2] + (width,), jnp.bfloat16)
    tile = 256
    tokens = tile // per
    for stream, chunk, one, two in ((0, mine, a0, b0), (1, other, a1, b1)):
        starts = start_ref[stream, 0:1, :]
        query_base = chunk * size + half * stream
        first_row = jnp.where(core == 0, half * stream, half * (1 - stream))
        need = jnp.min(starts) < (chunk - 2) * size

        @pl.when(need)
        def _():
            at = 0
            for step, ref, first, count in ((3, one, 0, size), (4, two, half * stream, size - half * stream)):
                load_keys(ref, None, first, count, cos_ref, sin_ref, base_ref, stream, step, None,
                          starts, (chunk - step) * size, query_base, keys, values, at)
                at += count

            def body(i, carry):
                r = pl.ds(pl.multiple_of(i * tile, tile), tile)
                parts = []
                for g in range(groups):
                    s = scores_of(qrot_ref[stream, g, r, :], pick[r, :], keys[g, :at, :])
                    before = max_ref[stream, g, r, :]
                    top = jnp.maximum(before, jnp.max(s, axis=1, keepdims=True))
                    p = jnp.exp2((s - top[:, :1]) * factor).astype(jnp.bfloat16)
                    scale = jnp.exp2((before - top) * factor)
                    new = jnp.dot(p, values[g, :at, :], preferred_element_type=jnp.float32)
                    old = acc_ref[stream, g, r, :]
                    o = (old[:, :width] * scale + new[:, :width]) / (old[:, width:] * scale + new[:, width:])
                    parts.append(o.reshape(tokens, per, width))
                out_ref[pl.ds(first_row + i * tokens, tokens)] = jnp.concatenate(parts, axis=1).astype(jnp.bfloat16)
                return carry

            lax.fori_loop(0, rows // tile, body, 0)

        @pl.when(jnp.logical_not(need))
        def _():
            def body(i, carry):
                r = pl.ds(pl.multiple_of(i * tile, tile), tile)
                parts = []
                for g in range(groups):
                    old = acc_ref[stream, g, r, :]
                    parts.append((old[:, :width] / old[:, width:]).reshape(tokens, per, width))
                out_ref[pl.ds(first_row + i * tokens, tokens)] = jnp.concatenate(parts, axis=1).astype(jnp.bfloat16)
                return carry

            lax.fori_loop(0, rows // tile, body, 0)


def shards(key_value, queries, doc_lengths):
    rows, groups, pair = key_value.shape
    width = pair // 2
    half = rows // 2
    heads = queries.shape[1]
    per = heads // groups
    factor = math.log2(math.e) / math.sqrt(width)
    vmem = pl.BlockSpec(memory_space=pltpu.VMEM)
    smem = pl.BlockSpec(memory_space=pltpu.SMEM)
    f32, bf16, i32 = jnp.float32, jnp.bfloat16, jnp.int32

    received = to_sibling(key_value)
    core = lax.rem(lax.axis_index("ctx"), 2)
    first = core * half
    second = (1 - core) * half

    def take(x, start):
        return lax.dynamic_slice_in_dim(x, start, half, 0)

    own = jnp.concatenate([take(key_value, first), take(received, first)], 0).transpose(1, 0, 2)
    own_other = jnp.concatenate([take(received, second), take(key_value, second)], 0).transpose(1, 0, 2)

    index = np.arange(width) % (width // 2)
    freq = jnp.asarray((ROPE_BASE ** (-(index * 2.0 / width))).astype(np.float32)[None, :])

    two = along_chain(own, 2)
    one = along_chain(own, 1)
    four = along_chain(two, 2)
    three = along_chain(one, 2)
    one_other, two_other, three_other, four_other = (to_sibling(x) for x in (one, two, three, four))

    shape = jax.ShapeDtypeStruct
    qrot, cos, sin, base, starts = pl.pallas_call(
        functools.partial(prepare_kernel, half),
        out_shape=(
            shape((2, groups, half * per, width), bf16),
            shape((rows, width), f32),
            shape((rows, width), f32),
            shape((4, 8, width), f32),
            shape((2, 8, half), i32),
        ),
        in_specs=[smem, vmem, vmem],
        out_specs=(vmem,) * 5,
        scratch_shapes=[pltpu.VMEM((2, half, 1, width), f32)],
        cost_estimate=pl.CostEstimate(flops=10 ** 8, bytes_accessed=2 * 10 ** 6, transcendentals=10 ** 5),
        name="prepare",
    )(doc_lengths, freq, queries)

    acc, top = pl.pallas_call(
        functools.partial(near_kernel, half, factor),
        out_shape=(
            shape((2, groups, half * per, 2 * width), f32),
            shape((2, groups, half * per, width), f32),
        ),
        in_specs=[vmem] * 11,
        out_specs=(vmem,) * 2,
        scratch_shapes=[
            pltpu.VMEM((groups, 3 * rows, 2 * width), bf16),
            pltpu.VMEM((groups, 3 * rows, 2 * width), bf16),
            pltpu.VMEM((half * per, half), bf16),
        ],
        cost_estimate=pl.CostEstimate(flops=3 * 10 ** 9, bytes_accessed=6 * 10 ** 6, transcendentals=3 * 10 ** 6),
        name="near",
    )(qrot, cos, sin, base, starts, own, own_other, one, one_other, two, two_other)

    return pl.pallas_call(
        functools.partial(far_kernel, half, factor),
        out_shape=shape((rows, heads, width), bf16),
        in_specs=[vmem] * 11,
        out_specs=vmem,
        scratch_shapes=[
            pltpu.VMEM((groups, 2 * rows, 2 * width), bf16),
            pltpu.VMEM((groups, 2 * rows, 2 * width), bf16),
            pltpu.VMEM((half * per, half), bf16),
        ],
        cost_estimate=pl.CostEstimate(flops=2 * 10 ** 9, bytes_accessed=6 * 10 ** 6, transcendentals=2 * 10 ** 6),
        name="far",
    )(qrot, cos, sin, base, starts, acc, top, three, three_other, four, four_other)


def solution(mesh):
    in_specs = (P("ctx", "tp", None), P("ctx", "tp", None), P())
    out_specs = P("ctx", "tp", None)
    return jax.shard_map(shards, mesh=mesh, in_specs=in_specs, out_specs=out_specs, check_vma=False)
```

time: 101 us -> 55.8 us (0.55)
  the two profiles are of different devices: /device:TPU:26 before, /device:TPU:29 now
where the time goes in v1:
time: 55.8 us; the launch traced here: 56.2 us
  Pallas kernels  34 us (61%)
  starting transfers between devices  12.5 us (22%)
  waiting for transfers between devices  6.15 us (11%)
  local copies, waits for them, and re-layouts  2.64 us (5%)
  other arithmetic  0.74 us (1%)
    pallas_call x1, Pallas kernels, shards(): pl.pallas_call(functools.partial(near_kernel, half, factor), out_shape=(s...  16.8 us
    pallas_call x1, Pallas kernels, shards(): pl.pallas_call(functools.partial(far_kernel, half, factor), out_shape=sha...  12.8 us
    ppermute x4, starting transfers between devices, along_chain(): return lax.ppermute(value, 'ctx', pairs)  8.04 us
    ppermute x4, waiting for transfers between devices, along_chain(): return lax.ppermute(value, 'ctx', pairs)  5 us
    ppermute x5, starting transfers between devices, to_sibling(): return lax.ppermute(value, 'ctx', [(i, i ^ 1) for i in range(count)])  4.47 us
    pallas_call x1, Pallas kernels, shards(): pl.pallas_call(functools.partial(prepare_kernel, half), out_shape=(shape(...  4.45 us
    unnamed x19, local copies, waits for them, and re-layouts  2.6 us
    ppermute x5, waiting for transfers between devices, to_sibling(): return lax.ppermute(value, 'ctx', [(i, i ^ 1) for i in range(count)])  1.15 us
  transfers between devices with their start and end apart: 9, of which 2 were waited for; matrix products, arithmetic and copies ran while one was open for 1% of the time, Pallas kernels for 38%

profile of v1, /device:TPU:29, one launch (start us, length us, event | category | flops | bytes accessed | tf_op | source)
XLA Modules:
  0.0 56.2 jit_solution(15319710572351787290)
XLA Ops:
  0.0 1.0 %copy.5 = bf16[256,2,256]{2,0,1:T(8,128)(2,1)S(1)} copy(bf16[256,2,256]{2,1,0:T(2,128)(2,1)} %param.4) | data formatting | bytes 524288 | tf_op args[0]
  1.0 0.7 %collective-permute-start = (bf16[256,2,256]{2,0,1:T(8,128)(2,1)S(1)}, bf16[256,2,256]{2,0,1:T(8,128)(2,1)S(1)}, u32[]{:S(2)}, u32[]{:S(2)}) collective-permute-start(bf16[256,2,256]{2,0,1:T(8,128)(2,1)S(1)} %copy.5), channel_id=1, source_target_pairs={{0,2},{2,0},{4,6},{6,4},{8,10},{10,8},{12,14},{14,12},{16,18},{18,... | collective-permute-start | bytes 786440 | tf_op jit(solution)/shard_map/ppermute | solution.py:32
  1.7 1.1 %collective-permute-done = bf16[256,2,256]{2,0,1:T(8,128)(2,1)S(1)} collective-permute-done((bf16[256,2,256]{2,0,1:T(8,128)(2,1)S(1)}, bf16[256,2,256]{2,0,1:T(8,128)(2,1)S(1)}, u32[]{:S(2)}, u32[]{:S(2)}) %collective-permute-start) | collective-permute-done | bytes 262176 | tf_op jit(solution)/shard_map/ppermute | solution.py:32
  2.9 0.0 copy-start.4
  2.9 2.1 %collective-permute-start.1 = (bf16[2,256,256]{2,1,0:T(8,128)(2,1)S(1)}, bf16[2,256,256]{2,1,0:T(8,128)(2,1)S(1)}, u32[]{:S(2)}, u32[]{:S(2)}) collective-permute-start(bf16[2,256,256]{2,1,0:T(8,128)(2,1)S(1)} %maximum_bitcast_fusion.own0), channel_id=1, source_target_pairs={{0,4},{4,8},{8,12},{12,16},{16,20},{20,24},{24,28},{28,30},{30,26}... | collective-permute-start | bytes 786440 | tf_op jit(solution)/shard_map/ppermute | solution.py:27
  5.1 2.1 %collective-permute-start.3 = (bf16[2,256,256]{2,1,0:T(8,128)(2,1)S(1)}, bf16[2,256,256]{2,1,0:T(8,128)(2,1)S(1)}, u32[]{:S(2)}, u32[]{:S(2)}) collective-permute-start(bf16[2,256,256]{2,1,0:T(8,128)(2,1)S(1)} %maximum_bitcast_fusion.own0), channel_id=1, source_target_pairs={{0,8},{4,12},{8,16},{12,20},{16,24},{20,28},{24,30},{28,26},{30,22... | collective-permute-start | bytes 786440 | tf_op jit(solution)/shard_map/ppermute | solution.py:27
  7.2 5.0 %collective-permute-done.1.a0 = bf16[2,256,256]{2,1,0:T(8,128)(2,1)S(1)} collective-permute-done((bf16[2,256,256]{2,1,0:T(8,128)(2,1)S(1)}, bf16[2,256,256]{2,1,0:T(8,128)(2,1)S(1)}, u32[]{:S(2)}, u32[]{:S(2)}) %collective-permute-start.1) | collective-permute-done | bytes 262176 | tf_op jit(solution)/shard_map/ppermute | solution.py:27
  12.2 0.0 copy-start.5
  12.2 1.9 %collective-permute-start.5 = (bf16[2,256,256]{2,1,0:T(8,128)(2,1)S(1)}, bf16[2,256,256]{2,1,0:T(8,128)(2,1)S(1)}, u32[]{:S(2)}, u32[]{:S(2)}) collective-permute-start(bf16[2,256,256]{2,1,0:T(8,128)(2,1)S(1)} %collective-permute-done.1.a0), channel_id=1, source_target_pairs={{0,8},{4,12},{8,16},{12,20},{16,24},{20,28},{24,30},{28,26},{30,22... | collective-permute-start | bytes 786440 | tf_op jit(solution)/shard_map/ppermute | solution.py:27
  14.1 0.0 collective-permute-done.3.b0
  14.1 0.0 copy-start.6
  14.1 1.9 %collective-permute-start.7 = (bf16[2,256,256]{2,1,0:T(8,128)(2,1)S(1)}, bf16[2,256,256]{2,1,0:T(8,128)(2,1)S(1)}, u32[]{:S(2)}, u32[]{:S(2)}) collective-permute-start(bf16[2,256,256]{2,1,0:T(8,128)(2,1)S(1)} %collective-permute-done.3.b0), channel_id=1, source_target_pairs={{0,8},{4,12},{8,16},{12,20},{16,24},{20,28},{24,30},{28,26},{30,22... | collective-permute-start | bytes 786440 | tf_op jit(solution)/shard_map/ppermute | solution.py:27
  16.0 2.6 %collective-permute-start.2 = (bf16[2,256,256]{2,1,0:T(8,128)(2,1)S(1)}, bf16[2,256,256]{2,1,0:T(8,128)(2,1)S(1)}, u32[]{:S(2)}, u32[]{:S(2)}) collective-permute-start(bf16[2,256,256]{2,1,0:T(8,128)(2,1)S(1)} %collective-permute-done.1.a0), channel_id=1, source_target_pairs={{0,2},{2,0},{4,6},{6,4},{8,10},{10,8},{12,14},{14,12},{16,18},{18,... | collective-permute-start | bytes 786440 | tf_op jit(solution)/shard_map/ppermute | solution.py:32
  18.7 0.1 collective-permute-start.4
  18.8 4.5 %prepare.1 = (bf16[2,2,1024,128]{3,2,1,0:T(8,128)(2,1)}, f32[256,128]{1,0:T(8,128)}, f32[256,128]{1,0:T(8,128)}, f32[4,8,128]{2,1,0:T(8,128)}, s32[2,8,128]{2,1,0:T(8,128)}) custom-call(s32[8]{0:T(128)} %docs_ref.1, f32[1,128]{1,0:T(1,128)} %constant.19.clone.freq_ref, bf16[256,16,128]{2,1,0:T(8,128)(2,1)} %q_ref.1), custom_call_target="tpu_custom_call" | custom-call | flops 100000000 | bytes 2000000 | tf_op jit(solution)/shard_map/prepare/pallas_call | solution.py:263
  23.2 0.7 %maximum_bitcast_fusion.1.own1 = bf16[2,256,256]{2,1,0:T(8,128)(2,1)} fusion(bf16[128,2,256]{2,0,1:T(8,128)(2,1)S(1)} %get-tuple-element.21, bf16[128,2,256]{2,0,1:T(8,128)(2,1)S(1)} %get-tuple-element.19), kind=kLoop, calls=%fused_computation.1 | loop fusion | flops 524288 | bytes 524288 | tf_op jit(solution)/shard_map/transpose | solution.py:251
  23.9 0.0 collective-permute-done.5.a0
  23.9 0.0 copy-start
  23.9 0.4 collective-permute-start.6
  24.4 0.0 collective-permute-done.7.b0
  24.4 0.0 copy-start.1
  24.4 0.6 %collective-permute-start.8 = (bf16[2,256,256]{2,1,0:T(8,128)(2,1)S(1)}, bf16[2,256,256]{2,1,0:T(8,128)(2,1)S(1)}, u32[]{:S(2)}, u32[]{:S(2)}) collective-permute-start(bf16[2,256,256]{2,1,0:T(8,128)(2,1)S(1)} %collective-permute-done.7.b0), channel_id=1, source_target_pairs={{0,2},{2,0},{4,6},{6,4},{8,10},{10,8},{12,14},{14,12},{16,18},{18,... | collective-permute-start | bytes 786440 | tf_op jit(solution)/shard_map/ppermute | solution.py:32
  25.0 0.0 collective-permute-done.2.a1
  25.0 0.0 copy-start.7
  25.0 0.0 collective-permute-done.4.b1
  25.0 0.0 copy-start.8
  25.0 0.0 copy-done.4
  25.0 0.0 copy-done.5
  25.0 0.0 copy-done.6
  25.0 0.7 %copy-done.7 = bf16[2,256,256]{2,1,0:T(8,128)(2,1)} copy-done((bf16[2,256,256]{2,1,0:T(8,128)(2,1)}, bf16[2,256,256]{2,1,0:T(8,128)(2,1)S(1)}, u32[]{:S(2)}) %copy-start.7) | copy-done | bytes 262168
  25.7 0.1 copy-done.8
  25.8 16.8 %near.1 = (f32[2,2,1024,256]{3,2,1,0:T(8,128)}, f32[2,2,1024,128]{3,2,1,0:T(8,128)}) custom-call(bf16[2,2,1024,128]{3,2,1,0:T(8,128)(2,1)} %get-tuple-element.12.qrot_ref, f32[256,128]{1,0:T(8,128)} %get-tuple-element.13.cos_ref, f32[256,128]{1,0:T(8,128)} %get-tuple-element.14.sin_ref, f32[4,8,128]{2,1,0:T(8,128)} %get-tuple-element.15.base_ref, ...), custom_call_target="tpu_custom_call" | custom-call | flops 3000000000 | bytes 6000000 | tf_op jit(solution)/shard_map/near/pallas_call | solution.py:279
  42.6 0.0 copy-done
  42.6 0.0 copy-done.1
  42.6 0.0 collective-permute-done.6.a1
  42.6 0.0 copy-start.2
  42.6 0.0 collective-permute-done.8.b1
  42.6 0.0 copy-start.3
  42.6 0.7 %copy-done.2 = bf16[2,256,256]{2,1,0:T(8,128)(2,1)} copy-done((bf16[2,256,256]{2,1,0:T(8,128)(2,1)}, bf16[2,256,256]{2,1,0:T(8,128)(2,1)S(1)}, u32[]{:S(2)}) %copy-start.2) | copy-done | bytes 262168
  43.3 0.1 copy-done.3
  43.4 12.8 %far.1 = bf16[256,16,128]{2,1,0:T(8,128)(2,1)} custom-call(bf16[2,2,1024,128]{3,2,1,0:T(8,128)(2,1)} %get-tuple-element.12.qrot_ref, f32[256,128]{1,0:T(8,128)} %get-tuple-element.13.cos_ref, f32[256,128]{1,0:T(8,128)} %get-tuple-element.14.sin_ref, f32[4,8,128]{2,1,0:T(8,128)} %get-tuple-element.15.base_ref, s32[2,8,128]{2,1,0:T(8,128)} %get-tuple-element.16.start_ref, ...), custom_call_target="tpu_custom_call" | custom-call | flops 2000000000 | bytes 6000000 | tf_op jit(solution)/shard_map/far/pallas_call | solution.py:296
  (3 shorter events, 0.1 us)
Async XLA Ops:
  1.0 1.9 %collective-permute-start = (bf16[256,2,256]{2,0,1:T(8,128)(2,1)S(1)}, bf16[256,2,256]{2,0,1:T(8,128)(2,1)S(1)}, u32[]{:S(2)}, u32[]{:S(2)}) collective-permute-start(bf16[256,2,256]{2,0,1:T(8,128)(2,1)S(1)} %copy.5), channel_id=1, source_target_pairs={{0,2},{2,0},{4,6},{6,4},{8,10},{10,8},{12,14},{14,12},{16,18},{18,... | collective-permute-start | bytes 786440 | tf_op jit(solution)/shard_map/ppermute | solution.py:32
  2.9 22.0 %copy-start.4 = (bf16[2,256,256]{2,1,0:T(8,128)(2,1)}, bf16[2,256,256]{2,1,0:T(8,128)(2,1)S(1)}, u32[]{:S(2)}) copy-start(bf16[2,256,256]{2,1,0:T(8,128)(2,1)S(1)} %maximum_bitcast_fusion.own0) | copy-start | bytes 786436
  2.9 9.2 %collective-permute-start.1 = (bf16[2,256,256]{2,1,0:T(8,128)(2,1)S(1)}, bf16[2,256,256]{2,1,0:T(8,128)(2,1)S(1)}, u32[]{:S(2)}, u32[]{:S(2)}) collective-permute-start(bf16[2,256,256]{2,1,0:T(8,128)(2,1)S(1)} %maximum_bitcast_fusion.own0), channel_id=1, source_target_pairs={{0,4},{4,8},{8,12},{12,16},{16,20},{20,24},{24,28},{28,30},{30,26}... | collective-permute-start | bytes 786440 | tf_op jit(solution)/shard_map/ppermute | solution.py:27
  5.1 9.0 %collective-permute-start.3 = (bf16[2,256,256]{2,1,0:T(8,128)(2,1)S(1)}, bf16[2,256,256]{2,1,0:T(8,128)(2,1)S(1)}, u32[]{:S(2)}, u32[]{:S(2)}) collective-permute-start(bf16[2,256,256]{2,1,0:T(8,128)(2,1)S(1)} %maximum_bitcast_fusion.own0), channel_id=1, source_target_pairs={{0,8},{4,12},{8,16},{12,20},{16,24},{20,28},{24,30},{28,26},{30,22... | collective-permute-start | bytes 786440 | tf_op jit(solution)/shard_map/ppermute | solution.py:27
  12.2 12.8 %copy-start.5 = (bf16[2,256,256]{2,1,0:T(8,128)(2,1)}, bf16[2,256,256]{2,1,0:T(8,128)(2,1)S(1)}, u32[]{:S(2)}) copy-start(bf16[2,256,256]{2,1,0:T(8,128)(2,1)S(1)} %collective-permute-done.1.a0) | copy-start | bytes 786436
  12.2 11.8 %collective-permute-start.5 = (bf16[2,256,256]{2,1,0:T(8,128)(2,1)S(1)}, bf16[2,256,256]{2,1,0:T(8,128)(2,1)S(1)}, u32[]{:S(2)}, u32[]{:S(2)}) collective-permute-start(bf16[2,256,256]{2,1,0:T(8,128)(2,1)S(1)} %collective-permute-done.1.a0), channel_id=1, source_target_pairs={{0,8},{4,12},{8,16},{12,20},{16,24},{20,28},{24,30},{28,26},{30,22... | collective-permute-start | bytes 786440 | tf_op jit(solution)/shard_map/ppermute | solution.py:27
  14.1 10.9 %copy-start.6 = (bf16[2,256,256]{2,1,0:T(8,128)(2,1)}, bf16[2,256,256]{2,1,0:T(8,128)(2,1)S(1)}, u32[]{:S(2)}) copy-start(bf16[2,256,256]{2,1,0:T(8,128)(2,1)S(1)} %collective-permute-done.3.b0) | copy-start | bytes 786436
  14.1 10.3 %collective-permute-start.7 = (bf16[2,256,256]{2,1,0:T(8,128)(2,1)S(1)}, bf16[2,256,256]{2,1,0:T(8,128)(2,1)S(1)}, u32[]{:S(2)}, u32[]{:S(2)}) collective-permute-start(bf16[2,256,256]{2,1,0:T(8,128)(2,1)S(1)} %collective-permute-done.3.b0), channel_id=1, source_target_pairs={{0,8},{4,12},{8,16},{12,20},{16,24},{20,28},{24,30},{28,26},{30,22... | collective-permute-start | bytes 786440 | tf_op jit(solution)/shard_map/ppermute | solution.py:27
  16.0 8.9 %collective-permute-start.2 = (bf16[2,256,256]{2,1,0:T(8,128)(2,1)S(1)}, bf16[2,256,256]{2,1,0:T(8,128)(2,1)S(1)}, u32[]{:S(2)}, u32[]{:S(2)}) collective-permute-start(bf16[2,256,256]{2,1,0:T(8,128)(2,1)S(1)} %collective-permute-done.1.a0), channel_id=1, source_target_pairs={{0,2},{2,0},{4,6},{6,4},{8,10},{10,8},{12,14},{14,12},{16,18},{18,... | collective-permute-start | bytes 786440 | tf_op jit(solution)/shard_map/ppermute | solution.py:32
  18.7 6.3 %collective-permute-start.4 = (bf16[2,256,256]{2,1,0:T(8,128)(2,1)S(1)}, bf16[2,256,256]{2,1,0:T(8,128)(2,1)S(1)}, u32[]{:S(2)}, u32[]{:S(2)}) collective-permute-start(bf16[2,256,256]{2,1,0:T(8,128)(2,1)S(1)} %collective-permute-done.3.b0), channel_id=1, source_target_pairs={{0,2},{2,0},{4,6},{6,4},{8,10},{10,8},{12,14},{14,12},{16,18},{18,... | collective-permute-start | bytes 786440 | tf_op jit(solution)/shard_map/ppermute | solution.py:32
  23.9 18.6 %copy-start = (bf16[2,256,256]{2,1,0:T(8,128)(2,1)}, bf16[2,256,256]{2,1,0:T(8,128)(2,1)S(1)}, u32[]{:S(2)}) copy-start(bf16[2,256,256]{2,1,0:T(8,128)(2,1)S(1)} %collective-permute-done.5.a0) | copy-start | bytes 786436
  23.9 18.6 %collective-permute-start.6 = (bf16[2,256,256]{2,1,0:T(8,128)(2,1)S(1)}, bf16[2,256,256]{2,1,0:T(8,128)(2,1)S(1)}, u32[]{:S(2)}, u32[]{:S(2)}) collective-permute-start(bf16[2,256,256]{2,1,0:T(8,128)(2,1)S(1)} %collective-permute-done.5.a0), channel_id=1, source_target_pairs={{0,2},{2,0},{4,6},{6,4},{8,10},{10,8},{12,14},{14,12},{16,18},{18,... | collective-permute-start | bytes 786440 | tf_op jit(solution)/shard_map/ppermute | solution.py:32
  24.4 18.2 %copy-start.1 = (bf16[2,256,256]{2,1,0:T(8,128)(2,1)}, bf16[2,256,256]{2,1,0:T(8,128)(2,1)S(1)}, u32[]{:S(2)}) copy-start(bf16[2,256,256]{2,1,0:T(8,128)(2,1)S(1)} %collective-permute-done.7.b0) | copy-start | bytes 786436
  24.4 18.2 %collective-permute-start.8 = (bf16[2,256,256]{2,1,0:T(8,128)(2,1)S(1)}, bf16[2,256,256]{2,1,0:T(8,128)(2,1)S(1)}, u32[]{:S(2)}, u32[]{:S(2)}) collective-permute-start(bf16[2,256,256]{2,1,0:T(8,128)(2,1)S(1)} %collective-permute-done.7.b0), channel_id=1, source_target_pairs={{0,2},{2,0},{4,6},{6,4},{8,10},{10,8},{12,14},{14,12},{16,18},{18,... | collective-permute-start | bytes 786440 | tf_op jit(solution)/shard_map/ppermute | solution.py:32
  25.0 0.7 %copy-start.7 = (bf16[2,256,256]{2,1,0:T(8,128)(2,1)}, bf16[2,256,256]{2,1,0:T(8,128)(2,1)S(1)}, u32[]{:S(2)}) copy-start(bf16[2,256,256]{2,1,0:T(8,128)(2,1)S(1)} %collective-permute-done.2.a1) | copy-start | bytes 786436
  25.0 0.8 %copy-start.8 = (bf16[2,256,256]{2,1,0:T(8,128)(2,1)}, bf16[2,256,256]{2,1,0:T(8,128)(2,1)S(1)}, u32[]{:S(2)}) copy-start(bf16[2,256,256]{2,1,0:T(8,128)(2,1)S(1)} %collective-permute-done.4.b1) | copy-start | bytes 786436
  42.6 0.8 %copy-start.2 = (bf16[2,256,256]{2,1,0:T(8,128)(2,1)}, bf16[2,256,256]{2,1,0:T(8,128)(2,1)S(1)}, u32[]{:S(2)}) copy-start(bf16[2,256,256]{2,1,0:T(8,128)(2,1)S(1)} %collective-permute-done.6.a1) | copy-start | bytes 786436
  42.6 0.8 %copy-start.3 = (bf16[2,256,256]{2,1,0:T(8,128)(2,1)}, bf16[2,256,256]{2,1,0:T(8,128)(2,1)S(1)}, u32[]{:S(2)}) copy-start(bf16[2,256,256]{2,1,0:T(8,128)(2,1)S(1)} %collective-permute-done.8.b1) | copy-start | bytes 786436

commit v2 on v0

v2 whole, which is shorter than its diff:
```python
import functools
import math

import jax
import jax.numpy as jnp
from jax import lax
from jax.experimental import pallas as pl
from jax.experimental.layout import Layout, with_layout_constraint
from jax.experimental.pallas import tpu as pltpu
from jax.sharding import PartitionSpec as P

ROPE_BASE = 500000.0
HIDDEN = -3.0e38
TILE = 256


def chain_device(chunk, chips):
    return 2 * chunk if chunk < chips else 2 * (2 * chips - 1 - chunk) + 1


def along_chain(value, steps):
    count = lax.axis_size("ctx")
    chips = count // 2
    pairs = [
        (chain_device(c, chips), chain_device(c + steps, chips)) for c in range(count - steps)
    ]
    return lax.ppermute(value, "ctx", pairs)


def to_sibling(value):
    count = lax.axis_size("ctx")
    return lax.ppermute(value, "ctx", [(i, i ^ 1) for i in range(count)])


def my_chunks():
    me = lax.axis_index("ctx")
    count = lax.axis_size("ctx")
    core = lax.rem(me, 2)
    chip = lax.div(me, 2)
    low, high = chip, count - 1 - chip
    mine = jnp.where(core == 0, low, high)
    other = jnp.where(core == 0, high, low)
    return core, (mine, other)


def first_row(core, stream, half):
    return jnp.where(core == 0, half * stream, half * (1 - stream))


def swap_halves(x):
    return pltpu.roll(x, x.shape[-1] // 2, axis=x.ndim - 1)


def load_keys(chunk_ref, first, count, tables, stream, step, chunk, causal, keys, values, at):
    cos_ref, sin_ref, base_ref, start_ref = tables
    size, width = cos_ref.shape
    half = start_ref.shape[-1]
    c = cos_ref[pl.ds(first, count), :]
    s = sin_ref[pl.ds(first, count), :]
    cosine = base_ref[stream, 0, step:step + 1, :] * c - base_ref[stream, 1, step:step + 1, :] * s
    sine = base_ref[stream, 2, step:step + 1, :] * c + base_ref[stream, 3, step:step + 1, :] * s
    offset = lax.broadcasted_iota(jnp.int32, (count, half), 0)
    visible = offset >= start_ref[stream, 0:1, :] - ((chunk - step) * size + first)
    if causal:
        query = lax.broadcasted_iota(jnp.int32, (count, half), 1) + half * stream
        visible = visible & (offset + first <= query)
    hidden = jnp.where(visible, 0.0, HIDDEN).astype(jnp.bfloat16)
    for g in range(keys.shape[0]):
        k = chunk_ref[g, pl.ds(first, count), :width].astype(jnp.float32)
        keys[g, pl.ds(at, count), :width] = (k * cosine + swap_halves(k) * sine).astype(jnp.bfloat16)
        keys[g, pl.ds(at, count), width:] = hidden
        values[g, pl.ds(at, count), :width] = chunk_ref[g, pl.ds(first, count), width:]


def fill_ones(values):
    width = values.shape[-1] // 2
    values[:, :, width:] = jnp.ones(values.shape[:2] + (width,), jnp.bfloat16)


def scores_of(q, pick, k):
    return lax.dot_general(
        jnp.concatenate([q, pick], axis=1), k, (((1,), (1,)), ((), ())),
        preferred_element_type=jnp.float32,
    )


def tables_kernel(half, docs_ref, freq_ref, q_hbm, q_ref, pick, cos_ref, sin_ref, base_ref, start_ref, arrived):
    core, chunks = my_chunks()
    size = 2 * half
    width = freq_ref.shape[-1]
    rows = pick.shape[0]
    per = rows // half
    load = pltpu.make_async_copy(q_hbm, q_ref, arrived)
    load.start()
    freq = freq_ref[...]
    angle = lax.broadcasted_iota(jnp.int32, (size, width), 0).astype(jnp.float32) * freq
    cos_ref[...] = jnp.cos(angle)
    sin_ref[...] = jnp.sin(angle)
    sign = jnp.where(lax.broadcasted_iota(jnp.int32, (1, width), 1) < width // 2, -1.0, 1.0)
    step = lax.broadcasted_iota(jnp.int32, (8, width), 0)
    for stream in range(2):
        place = ((chunks[stream] - step) * size).astype(jnp.float32) * freq
        base_cos = jnp.cos(place)
        base_sin = jnp.sin(place)
        base_ref[stream, 0] = base_cos
        base_ref[stream, 1] = base_sin
        base_ref[stream, 2] = base_sin * sign
        base_ref[stream, 3] = base_cos * sign
    lanes = lax.broadcasted_iota(jnp.int32, (8, half), 1)
    places = [chunks[stream] * size + half * stream + lanes for stream in range(2)]

    def doc_step(i, carry):
        end, first, second = carry
        end = end + docs_ref[i]
        return end, jnp.where(places[0] >= end, end, first), jnp.where(places[1] >= end, end, second)

    zero = jnp.zeros((8, half), jnp.int32)
    _, first, second = lax.fori_loop(0, docs_ref.shape[0], doc_step, (jnp.int32(0), zero, zero))
    start_ref[0] = first
    start_ref[1] = second
    token = lax.broadcasted_iota(jnp.int32, (rows, half), 0) // per
    lane = lax.broadcasted_iota(jnp.int32, (rows, half), 1)
    pick[...] = jnp.where(token == lane, 1.0, 0.0).astype(jnp.bfloat16)
    load.wait()


def begin_kernel(half, factor, q_ref, pick, cos_ref, sin_ref, base_ref, start_ref, own0, own1,
                 qrot_ref, acc0, top0, acc1, top1, work, keys, values):
    core, chunks = my_chunks()
    groups, rows, width = qrot_ref.shape[1:]
    per = rows // half
    fill_ones(values)
    tables = (cos_ref, sin_ref, base_ref, start_ref)
    tokens = 16
    for stream, own, acc, top in ((0, own0, acc0, top0), (1, own1, acc1, top1)):
        c = cos_ref[pl.ds(half * stream, half), :]
        s = sin_ref[pl.ds(half * stream, half), :]
        work[0] = (base_ref[stream, 0, 0:1, :] * c - base_ref[stream, 1, 0:1, :] * s)[:, None, :]
        work[1] = (base_ref[stream, 2, 0:1, :] * c + base_ref[stream, 3, 0:1, :] * s)[:, None, :]
        count = half * (1 + stream)
        load_keys(own, 0, count, tables, stream, 0, chunks[stream], True, keys, values, 0)
        base_row = first_row(core, stream, half)

        def rope_step(i, carry):
            at = i * tokens
            x = q_ref[pl.ds(base_row + at, tokens)].astype(jnp.float32)
            y = x * work[0, pl.ds(at, tokens)] + swap_halves(x) * work[1, pl.ds(at, tokens)]
            for g in range(groups):
                piece = y[:, g * per:(g + 1) * per, :].reshape(tokens * per, width)
                r = pl.ds(pl.multiple_of(at * per, tokens * per), tokens * per)
                qrot_ref[stream, g, r, :] = piece.astype(jnp.bfloat16)
            return carry

        lax.fori_loop(0, half // tokens, rope_step, 0)

        def body(i, carry):
            for u in range(2):
                for g in range(groups):
                    r = pl.ds(pl.multiple_of((2 * i + u) * TILE, TILE), TILE)
                    x = scores_of(qrot_ref[stream, g, r, :], pick[r, :], keys[g, :count, :])
                    high = jnp.max(x, axis=1, keepdims=True)
                    p = jnp.exp2((x - high) * factor).astype(jnp.bfloat16)
                    acc[g, r, :] = jnp.dot(p, values[g, :count, :], preferred_element_type=jnp.float32)
                    top[g, r, :] = jnp.broadcast_to(high, (TILE, width))
            return carry

        lax.fori_loop(0, rows // (2 * TILE), body, 0)


def update(factor, q, pick, k, v, acc, before):
    width = before.shape[-1]
    x = scores_of(q, pick, k)
    top = jnp.maximum(before, jnp.max(x, axis=1, keepdims=True))
    p = jnp.exp2((x - top[:, :1]) * factor).astype(jnp.bfloat16)
    scale = jnp.exp2((before - top) * factor)
    new = jnp.dot(p, v, preferred_element_type=jnp.float32)
    return acc[:, :width] * scale + new[:, :width], acc[:, width:] * scale + new[:, width:], top


def middle_kernel(half, factor, stream, qrot_ref, pick, cos_ref, sin_ref, base_ref, start_ref, old_acc, old_top, pair_ref,
                  acc_ref, top_ref, keys, values):
    core, chunks = my_chunks()
    chunk = chunks[stream]
    size = 2 * half
    groups, rows, width = qrot_ref.shape[1:]
    tables = (cos_ref, sin_ref, base_ref, start_ref)
    earliest = jnp.min(start_ref[stream])

    def work(chunks_used):
        fill_ones(values)
        for n in range(chunks_used):
            load_keys(pair_ref.at[n], 0, size, tables, stream, 1 + n, chunk, False, keys, values, n * size)
        count = chunks_used * size

        def body(i, carry):
            for u in range(2):
                for g in range(groups):
                    r = pl.ds(pl.multiple_of((2 * i + u) * TILE, TILE), TILE)
                    first, second, top = update(
                        factor, qrot_ref[stream, g, r, :], pick[r, :], keys[g, :count, :], values[g, :count, :],
                        old_acc[g, r, :], old_top[g, r, :])
                    acc_ref[g, r, :width] = first
                    acc_ref[g, r, width:] = second
                    top_ref[g, r, :] = top
            return carry

        lax.fori_loop(0, rows // (2 * TILE), body, 0)

    far = earliest < (chunk - 1) * size
    close = earliest < chunk * size
    pl.when(far)(lambda: work(2))
    pl.when(close & jnp.logical_not(far))(lambda: work(1))


def end_kernel(half, factor, stream, qrot_ref, pick, cos_ref, sin_ref, base_ref, start_ref, acc_ref, top_ref, pair_ref, *refs):
    out_hbm, keys, values, result, sent = refs[-5:]
    core, chunks = my_chunks()
    chunk = chunks[stream]
    size = 2 * half
    groups, rows, width = qrot_ref.shape[1:]
    per = rows // half
    tokens = TILE // per
    tables = (cos_ref, sin_ref, base_ref, start_ref)
    earliest = jnp.min(start_ref[stream])
    base_row = first_row(core, stream, half)

    def send(part):
        span = half // 2
        return pltpu.make_async_copy(
            result.at[pl.ds(part * span, span)], out_hbm.at[pl.ds(base_row + part * span, span)], sent.at[part])

    def finish(one):
        def body(i, carry):
            for u in range(2):
                at = 2 * i + u
                r = pl.ds(pl.multiple_of(at * TILE, TILE), TILE)
                parts = []
                for g in range(groups):
                    first, second = one(g, r)
                    parts.append((first / second).reshape(tokens, per, width))
                result[pl.ds(at * tokens, tokens)] = jnp.concatenate(parts, axis=1).astype(jnp.bfloat16)
            send(i).start()
            return carry

        lax.fori_loop(0, rows // (2 * TILE), body, 0)

    def work(chunks_used):
        fill_ones(values)
        used = 0
        for n in range(chunks_used):
            begin = half * stream if n == 1 else 0
            load_keys(pair_ref.at[n], begin, size - begin, tables, stream, 3 + n, chunk, False, keys, values, used)
            used += size - begin

        def one(g, r):
            first, second, _ = update(
                factor, qrot_ref[stream, g, r, :], pick[r, :], keys[g, :used, :], values[g, :used, :],
                acc_ref[g, r, :], top_ref[g, r, :])
            return first, second

        finish(one)

    far = earliest < (chunk - 3) * size
    close = earliest < (chunk - 2) * size
    pl.when(far)(lambda: work(2))
    pl.when(close & jnp.logical_not(far))(lambda: work(1))
    pl.when(jnp.logical_not(close))(lambda: finish(lambda g, r: (acc_ref[g, r, :width], acc_ref[g, r, width:])))
    send(0).wait()
    send(1).wait()


def shards(key_value, queries, doc_lengths):
    rows, groups, pair = key_value.shape
    width = pair // 2
    half = rows // 2
    heads = queries.shape[1]
    per = heads // groups
    factor = math.log2(math.e) / math.sqrt(width)
    vmem = pl.BlockSpec(memory_space=pltpu.VMEM)
    smem = pl.BlockSpec(memory_space=pltpu.SMEM)
    hbm = pl.BlockSpec(memory_space=pltpu.HBM)
    f32, bf16, i32 = jnp.float32, jnp.bfloat16, jnp.int32
    local = pltpu.VMEM
    params = pltpu.CompilerParams(vmem_limit_bytes=16 << 20)

    def near(*values):
        return [pltpu.with_memory_space_constraint(x, pltpu.VMEM) for x in values]

    index = (jnp.arange(width, dtype=jnp.int32) % (width // 2)).astype(f32)
    freq = (ROPE_BASE ** (-(index * 2.0 / width)))[None, :]
    received = with_layout_constraint(to_sibling(key_value), Layout((0, 1, 2)))
    q, *tables = pl.pallas_call(
        functools.partial(tables_kernel, half),
        out_shape=(
            local((rows, heads, width), bf16),
            local((half * per, half), bf16),
            local((rows, width), f32),
            local((rows, width), f32),
            local((2, 4, 8, width), f32),
            local((2, 8, half), i32),
        ),
        in_specs=[smem, vmem, hbm],
        out_specs=(vmem,) * 6,
        scratch_shapes=[pltpu.SemaphoreType.DMA(())],
        cost_estimate=pl.CostEstimate(flops=10 ** 7, bytes_accessed=10 ** 6, transcendentals=10 ** 5),
        compiler_params=params,
        name="tables",
    )(doc_lengths, *near(freq), queries)
    received, q = lax.optimization_barrier((received, q))
    core = lax.rem(lax.axis_index("ctx"), 2)
    first = core * half
    second = (1 - core) * half

    def take(x, start):
        return lax.dynamic_slice_in_dim(x, start, half, 0)

    own = jnp.concatenate([take(key_value, first), take(received, first)], 0).transpose(1, 0, 2)
    own_other = jnp.concatenate([take(received, second), take(key_value, second)], 0).transpose(1, 0, 2)

    one = along_chain(own, 1)
    two = along_chain(own, 2)

    state = (local((groups, half * per, 2 * width), f32), local((groups, half * per, width), f32))
    key_scratch = [pltpu.VMEM((groups, 2 * rows, 2 * width), bf16), pltpu.VMEM((groups, 2 * rows, 2 * width), bf16)]
    qrot, acc0, top0, acc1, top1 = pl.pallas_call(
        functools.partial(begin_kernel, half, factor),
        out_shape=(local((2, groups, half * per, width), bf16),) + state + state,
        in_specs=[vmem] * 8,
        out_specs=(vmem,) * 5,
        scratch_shapes=[
            pltpu.VMEM((2, half, 1, width), f32),
            pltpu.VMEM((groups, rows, 2 * width), bf16),
            pltpu.VMEM((groups, rows, 2 * width), bf16),
        ],
        cost_estimate=pl.CostEstimate(flops=2 * 10 ** 9, bytes_accessed=10 ** 6, transcendentals=10 ** 6),
        compiler_params=params,
        name="begin",
    )(*near(q, *tables, own, own_other))
    tables = [qrot] + tables

    near_pair = jnp.stack([one, two])
    near_pair, acc0, acc1 = lax.optimization_barrier((near_pair, acc0, acc1))
    far_pair = along_chain(near_pair, 2)
    near_other = to_sibling(near_pair)

    def middle(stream, acc, top, keys):
        return pl.pallas_call(
            functools.partial(middle_kernel, half, factor, stream),
            out_shape=state,
            in_specs=[vmem] * 9,
            out_specs=(vmem,) * 2,
            scratch_shapes=key_scratch,
            input_output_aliases={6: 0, 7: 1},
            cost_estimate=pl.CostEstimate(flops=10 ** 9, bytes_accessed=10 ** 6, transcendentals=10 ** 6),
            compiler_params=params,
            name="middle%d" % stream,
        )(*near(*tables, acc, top, keys))

    acc0, top0 = middle(0, acc0, top0, near_pair)
    acc1, top1 = middle(1, acc1, top1, near_other)

    far_pair, acc0, acc1 = lax.optimization_barrier((far_pair, acc0, acc1))
    far_other = to_sibling(far_pair)

    def end(stream, acc, top, keys, *out):
        return pl.pallas_call(
            functools.partial(end_kernel, half, factor, stream),
            out_shape=pltpu.HBM((rows, heads, width), bf16),
            in_specs=[vmem] * 9 + [hbm] * len(out),
            out_specs=hbm,
            scratch_shapes=key_scratch + [pltpu.VMEM((half, heads, width), bf16), pltpu.SemaphoreType.DMA((2,))],
            input_output_aliases={9: 0} if out else {},
            cost_estimate=pl.CostEstimate(flops=10 ** 9, bytes_accessed=10 ** 6, transcendentals=10 ** 6),
            compiler_params=params,
            name="end%d" % stream,
        )(*near(*tables, acc, top, keys), *out)

    out = end(0, acc0, top0, far_pair)
    return end(1, acc1, top1, far_other, out)


def solution(mesh):
    in_specs = (P("ctx", "tp", None), P("ctx", "tp", None), P())
    out_specs = P("ctx", "tp", None)
    return jax.shard_map(shards, mesh=mesh, in_specs=in_specs, out_specs=out_specs, check_vma=False)
```

time: 101 us -> 36.5 us (0.36)
  the two profiles are of different devices: /device:TPU:26 before, /device:TPU:29 now
where the time goes in v2:
time: 36.5 us; the launch traced here: 36.7 us
  Pallas kernels  21.4 us (59%)
  starting transfers between devices  9.38 us (26%)
  local copies, waits for them, and re-layouts  3.11 us (9%)
  waiting for transfers between devices  2.45 us (7%)
    ppermute x3, starting transfers between devices, along_chain(): return lax.ppermute(value, 'ctx', pairs)  8.23 us
    pallas_call x2, Pallas kernels, end(): pl.pallas_call(functools.partial(end_kernel, half, factor, stream), out_s...  8.06 us
    pallas_call x2, Pallas kernels, middle(): pl.pallas_call(functools.partial(middle_kernel, half, factor, stream), ou...  6.77 us
    pallas_call x1, Pallas kernels, shards(): pl.pallas_call(functools.partial(begin_kernel, half, factor), out_shape=(...  5.26 us
    ppermute x3, waiting for transfers between devices, along_chain(): return lax.ppermute(value, 'ctx', pairs)  2.44 us
    unnamed x6, local copies, waits for them, and re-layouts  1.91 us
    pallas_call x1, Pallas kernels, shards(): pl.pallas_call(functools.partial(tables_kernel, half), out_shape=(local((...  1.28 us
    dynamic_slice x2, local copies, waits for them, and re-layouts, take(): return lax.dynamic_slice_in_dim(x, start, half, 0)  1.18 us
  transfers between devices with their start and end apart: 6, of which 2 were waited for; matrix products, arithmetic and copies ran while one was open for 3% of the time, Pallas kernels for 48%

profile of v2, /device:TPU:29, one launch (start us, length us, event | category | flops | bytes accessed | tf_op | source)
XLA Modules:
  0.0 36.7 jit_solution(1299795433086827886)
XLA Ops:
  0.0 0.7 %collective-permute-start = (bf16[256,2,256]{2,1,0:T(2,128)(2,1)}, bf16[256,2,256]{2,1,0:T(2,128)(2,1)S(1)}, u32[]{:S(2)}, u32[]{:S(2)}) collective-permute-start(bf16[256,2,256]{2,1,0:T(2,128)(2,1)} %param.3), channel_id=1, source_target_pairs={{0,2},{2,0},{4,6},{6,4},{8,10},{10,8},{12,14},{14,12},{16,18},{18,... | collective-permute-start | bytes 786440 | tf_op jit(solution)/shard_map/ppermute | solution.py:32
  0.7 1.1 %constant_dynamic-slice_fusion = (bf16[128,2,256]{2,1,0:T(2,128)(2,1)S(1)}, bf16[128,2,256]{2,1,0:T(2,128)(2,1)S(1)}) fusion(bf16[256,2,256]{2,1,0:T(2,128)(2,1)} %param.3, s32[]{:T(128)S(6)} %select_n.24, s32[]{:T(128)S(6)} %select_n.23), kind=kLoop, calls=%fused_computation.4 | loop fusion | bytes 524296 | tf_op jit(solution)/shard_map/dynamic_slice | solution.py:315
  1.9 0.0 copy-start
  1.9 1.2 %copy-done = bf16[256,16,128]{2,1,0:T(8,128)(2,1)S(1)} copy-done((bf16[256,16,128]{2,1,0:T(8,128)(2,1)S(1)}, bf16[256,16,128]{2,1,0:T(8,128)(2,1)}, u32[]{:S(2)}) %copy-start) | copy-done | bytes 1048600
  3.1 0.0 copy-start.1
  3.1 0.7 %copy-done.1 = s32[8]{0:T(128)S(1)} copy-done((s32[8]{0:T(128)S(1)}, s32[8]{0:T(128)}, u32[]{:S(2)}) %copy-start.1) | copy-done | bytes 56
  3.8 1.3 %tables.1 = (bf16[256,16,128]{2,1,0:T(8,128)(2,1)S(1)}, bf16[1024,128]{1,0:T(8,128)(2,1)S(1)}, f32[256,128]{1,0:T(8,128)S(1)}, f32[256,128]{1,0:T(8,128)S(1)}, f...) custom-call(s32[8]{0:T(128)S(1)} %copy-done.1, f32[1,128]{1,0:T(1,128)S(1)} %fusion.3.freq_ref, ...), custom_call_target="tpu_custom_call" | custom-call | flops 10000000 | bytes 1000000 | tf_op jit(solution)/shard_map/tables/pallas_call | solution.py:292
  5.1 0.0 collective-permute-done
  5.2 2.1 %collective-permute-start.2 = (bf16[2,256,256]{2,1,0:T(8,128)(2,1)S(1)}, bf16[2,256,256]{2,1,0:T(8,128)(2,1)S(1)}, u32[]{:S(2)}, u32[]{:S(2)}) collective-permute-start(bf16[2,256,256]{2,1,0:T(8,128)(2,1)S(1)} %maximum_bitcast_fusion.own0), channel_id=1, source_target_pairs={{0,8},{4,12},{8,16},{12,20},{16,24},{20,28},{24,30},{28,26},{30,22... | collective-permute-start | bytes 786440 | tf_op jit(solution)/shard_map/ppermute | solution.py:27
  7.3 2.1 %collective-permute-start.1 = (bf16[2,256,256]{2,1,0:T(8,128)(2,1)S(1)}, bf16[2,256,256]{2,1,0:T(8,128)(2,1)S(1)}, u32[]{:S(2)}, u32[]{:S(2)}) collective-permute-start(bf16[2,256,256]{2,1,0:T(8,128)(2,1)S(1)} %maximum_bitcast_fusion.own0), channel_id=1, source_target_pairs={{0,4},{4,8},{8,12},{12,16},{16,20},{20,24},{24,28},{28,30},{30,26}... | collective-permute-start | bytes 786440 | tf_op jit(solution)/shard_map/ppermute | solution.py:27
  9.4 5.3 %begin.1 = (bf16[2,2,1024,128]{3,2,1,0:T(8,128)(2,1)S(1)}, f32[2,1024,256]{2,1,0:T(8,128)S(1)}, f32[2,1024,128]{2,1,0:T(8,128)S(1)}, f32[2,1024,256]{2,1,0:T(8,128)S(1)}, f32[2,1024,128]{2,1,0:T(8,128)S(1)}) custom-call(bf16[256,16,128]{2,1,0:T(8,128)(2,1)S(1)} %get-tuple-element.29.q_ref, bf16[1024,128]{1,0:T(8,128)(2,1)S(1)} %get-tuple-element.30.pick, ...), custom_call_target="tpu_custom_call" | custom-call | flops 2000000000 | bytes 1000000 | tf_op jit(solution)/shard_map/begin/pallas_call | solution.py:325
  14.7 0.0 collective-permute-done.2
  14.7 2.1 %collective-permute-done.1 = bf16[2,256,256]{2,1,0:T(8,128)(2,1)S(1)} collective-permute-done((bf16[2,256,256]{2,1,0:T(8,128)(2,1)S(1)}, bf16[2,256,256]{2,1,0:T(8,128)(2,1)S(1)}, u32[]{:S(2)}, u32[]{:S(2)}) %collective-permute-start.1) | collective-permute-done | bytes 262176 | tf_op jit(solution)/shard_map/ppermute | solution.py:27
  16.8 0.1 pad_maximum_fusion.pair_ref
  16.9 0.1 collective-permute-start.4
  16.9 4.0 %collective-permute-start.3 = (bf16[2,2,256,256]{3,2,1,0:T(8,128)(2,1)S(1)}, bf16[2,2,256,256]{3,2,1,0:T(8,128)(2,1)S(1)}, u32[]{:S(2)}, u32[]{:S(2)}) collective-permute-start(bf16[2,2,256,256]{3,2,1,0:T(8,128)(2,1)S(1)} %pad_maximum_fusion.pair_ref), channel_id=1, source_target_pairs={{0,8},{4,12},{8,16},{12,20},{16,24},{20,28},{24,30},{28,26},{30,22... | collective-permute-start | bytes 1572872 | tf_op jit(solution)/shard_map/ppermute | solution.py:27
  21.0 3.4 %middle0.1 = (f32[2,1024,256]{2,1,0:T(8,128)S(1)}, f32[2,1024,128]{2,1,0:T(8,128)S(1)}) custom-call(bf16[2,2,1024,128]{3,2,1,0:T(8,128)(2,1)S(1)} %get-tuple-element.36.qrot_ref, bf16[1024,128]{1,0:T(8,128)(2,1)S(1)} %get-tuple-element.30.pick, f32[256,128]{1,0:T(8,128)S(1)} %get-tuple-element.31.cos_ref, ...), custom_call_target="tpu_custom_call", output_to_operand_aliasing={{0}: (6, {}), {1}: (7, {})} | custom-call | flops 1000000000 | bytes 1000000 | tf_op jit(solution)/shard_map/middle0/pallas_call | solution.py:347
  24.4 0.0 collective-permute-done.4.pair_ref
  24.4 3.4 %middle1.1 = (f32[2,1024,256]{2,1,0:T(8,128)S(1)}, f32[2,1024,128]{2,1,0:T(8,128)S(1)}) custom-call(bf16[2,2,1024,128]{3,2,1,0:T(8,128)(2,1)S(1)} %get-tuple-element.36.qrot_ref, bf16[1024,128]{1,0:T(8,128)(2,1)S(1)} %get-tuple-element.30.pick, f32[256,128]{1,0:T(8,128)S(1)} %get-tuple-element.31.cos_ref, ...), custom_call_target="tpu_custom_call", output_to_operand_aliasing={{0}: (6, {}), {1}: (7, {})} | custom-call | flops 1000000000 | bytes 1000000 | tf_op jit(solution)/shard_map/middle1/pallas_call | solution.py:347
  27.8 0.3 collective-permute-done.3.pair_ref
  28.1 0.4 %collective-permute-start.5 = (bf16[2,2,256,256]{3,2,1,0:T(8,128)(2,1)S(1)}, bf16[2,2,256,256]{3,2,1,0:T(8,128)(2,1)S(1)}, u32[]{:S(2)}, u32[]{:S(2)}) collective-permute-start(bf16[2,2,256,256]{3,2,1,0:T(8,128)(2,1)S(1)} %collective-permute-done.3.pair_ref), channel_id=1, source_target_pairs={{0,2},{2,0},{4,6},{6,4},{8,10},{10,8},{12,14},{14,12},{16,18},{18,... | collective-permute-start | bytes 1572872 | tf_op jit(solution)/shard_map/ppermute | solution.py:32
  28.5 4.2 %end0.1.refs_0_ = bf16[256,16,128]{2,1,0:T(8,128)(2,1)} custom-call(bf16[2,2,1024,128]{3,2,1,0:T(8,128)(2,1)S(1)} %get-tuple-element.36.qrot_ref, bf16[1024,128]{1,0:T(8,128)(2,1)S(1)} %get-tuple-element.30.pick, f32[256,128]{1,0:T(8,128)S(1)} %get-tuple-element.31.cos_ref, f32[256,128]{1,0:T(8,128)S(1)} %get-tuple-element.32.sin_ref, ...), custom_call_target="tpu_custom_call" | custom-call | flops 1000000000 | bytes 1000000 | tf_op jit(solution)/shard_map/end0/pallas_call | solution.py:366
  32.7 0.0 collective-permute-done.5.pair_ref
  32.7 3.9 %end1.1 = bf16[256,16,128]{2,1,0:T(8,128)(2,1)} custom-call(bf16[2,2,1024,128]{3,2,1,0:T(8,128)(2,1)S(1)} %get-tuple-element.36.qrot_ref, bf16[1024,128]{1,0:T(8,128)(2,1)S(1)} %get-tuple-element.30.pick, f32[256,128]{1,0:T(8,128)S(1)} %get-tuple-element.31.cos_ref, f32[256,128]{1,0:T(8,128)S(1)} %get-tuple-element.32.sin_ref, ...), custom_call_target="tpu_custom_call", output_to_operand_aliasing={{}: (9, {})} | custom-call | flops 1000000000 | bytes 1000000 | tf_op jit(solution)/shard_map/end1/pallas_call | solution.py:366
  (7 shorter events, 0.1 us)
Async XLA Ops:
  0.0 5.1 %collective-permute-start = (bf16[256,2,256]{2,1,0:T(2,128)(2,1)}, bf16[256,2,256]{2,1,0:T(2,128)(2,1)S(1)}, u32[]{:S(2)}, u32[]{:S(2)}) collective-permute-start(bf16[256,2,256]{2,1,0:T(2,128)(2,1)} %param.3), channel_id=1, source_target_pairs={{0,2},{2,0},{4,6},{6,4},{8,10},{10,8},{12,14},{14,12},{16,18},{18,... | collective-permute-start | bytes 786440 | tf_op jit(solution)/shard_map/ppermute | solution.py:32
  1.9 1.2 %copy-start = (bf16[256,16,128]{2,1,0:T(8,128)(2,1)S(1)}, bf16[256,16,128]{2,1,0:T(8,128)(2,1)}, u32[]{:S(2)}) copy-start(bf16[256,16,128]{2,1,0:T(8,128)(2,1)} %q_hbm.1) | copy-start | bytes 3145732
  3.1 0.7 %copy-start.1 = (s32[8]{0:T(128)S(1)}, s32[8]{0:T(128)}, u32[]{:S(2)}) copy-start(s32[8]{0:T(128)} %docs_ref.1) | copy-start | bytes 100
  5.2 9.5 %collective-permute-start.2 = (bf16[2,256,256]{2,1,0:T(8,128)(2,1)S(1)}, bf16[2,256,256]{2,1,0:T(8,128)(2,1)S(1)}, u32[]{:S(2)}, u32[]{:S(2)}) collective-permute-start(bf16[2,256,256]{2,1,0:T(8,128)(2,1)S(1)} %maximum_bitcast_fusion.own0), channel_id=1, source_target_pairs={{0,8},{4,12},{8,16},{12,20},{16,24},{20,28},{24,30},{28,26},{30,22... | collective-permute-start | bytes 786440 | tf_op jit(solution)/shard_map/ppermute | solution.py:27
  7.3 9.5 %collective-permute-start.1 = (bf16[2,256,256]{2,1,0:T(8,128)(2,1)S(1)}, bf16[2,256,256]{2,1,0:T(8,128)(2,1)S(1)}, u32[]{:S(2)}, u32[]{:S(2)}) collective-permute-start(bf16[2,256,256]{2,1,0:T(8,128)(2,1)S(1)} %maximum_bitcast_fusion.own0), channel_id=1, source_target_pairs={{0,4},{4,8},{8,12},{12,16},{16,20},{20,24},{24,28},{28,30},{30,26}... | collective-permute-start | bytes 786440 | tf_op jit(solution)/shard_map/ppermute | solution.py:27
  16.9 7.5 %collective-permute-start.4 = (bf16[2,2,256,256]{3,2,1,0:T(8,128)(2,1)S(1)}, bf16[2,2,256,256]{3,2,1,0:T(8,128)(2,1)S(1)}, u32[]{:S(2)}, u32[]{:S(2)}) collective-permute-start(bf16[2,2,256,256]{3,2,1,0:T(8,128)(2,1)S(1)} %pad_maximum_fusion.pair_ref), channel_id=1, source_target_pairs={{0,2},{2,0},{4,6},{6,4},{8,10},{10,8},{12,14},{14,12},{16,18},{18,... | collective-permute-start | bytes 1572872 | tf_op jit(solution)/shard_map/ppermute | solution.py:32
  16.9 11.2 %collective-permute-start.3 = (bf16[2,2,256,256]{3,2,1,0:T(8,128)(2,1)S(1)}, bf16[2,2,256,256]{3,2,1,0:T(8,128)(2,1)S(1)}, u32[]{:S(2)}, u32[]{:S(2)}) collective-permute-start(bf16[2,2,256,256]{3,2,1,0:T(8,128)(2,1)S(1)} %pad_maximum_fusion.pair_ref), channel_id=1, source_target_pairs={{0,8},{4,12},{8,16},{12,20},{16,24},{20,28},{24,30},{28,26},{30,22... | collective-permute-start | bytes 1572872 | tf_op jit(solution)/shard_map/ppermute | solution.py:27
  28.1 4.6 %collective-permute-start.5 = (bf16[2,2,256,256]{3,2,1,0:T(8,128)(2,1)S(1)}, bf16[2,2,256,256]{3,2,1,0:T(8,128)(2,1)S(1)}, u32[]{:S(2)}, u32[]{:S(2)}) collective-permute-start(bf16[2,2,256,256]{3,2,1,0:T(8,128)(2,1)S(1)} %collective-permute-done.3.pair_ref), channel_id=1, source_target_pairs={{0,2},{2,0},{4,6},{6,4},{8,10},{10,8},{12,14},{14,12},{16,18},{18,... | collective-permute-start | bytes 1572872 | tf_op jit(solution)/shard_map/ppermute | solution.py:32

commit v3 on v2

--- a/solution.py
+++ b/solution.py
@@ -8,6 +8,7 @@
 from jax.experimental.layout import Layout, with_layout_constraint
 from jax.experimental.pallas import tpu as pltpu
 from jax.sharding import PartitionSpec as P
+
 
 ROPE_BASE = 500000.0
 HIDDEN = -3.0e38
@@ -84,14 +85,19 @@
     )
 
 
-def tables_kernel(half, docs_ref, freq_ref, q_hbm, q_ref, pick, cos_ref, sin_ref, base_ref, start_ref, arrived):
-    core, chunks = my_chunks()
+def tables_kernel(half, freq_ref, docs_hbm, kv_hbm, q_hbm, kv_ref, q_ref, pick, cos_ref, sin_ref, base_ref, start_ref, docs_ref, arrived):
+    _, chunks = my_chunks()
     size = 2 * half
     width = freq_ref.shape[-1]
     rows = pick.shape[0]
     per = rows // half
-    load = pltpu.make_async_copy(q_hbm, q_ref, arrived)
-    load.start()
+    loads = [
+        pltpu.make_async_copy(docs_hbm, docs_ref, arrived.at[0]),
+        pltpu.make_async_copy(kv_hbm, kv_ref, arrived.at[1]),
+        pltpu.make_async_copy(q_hbm, q_ref, arrived.at[2]),
+    ]
+    for load in loads:
+        load.start()
     freq = freq_ref[...]
     angle = lax.broadcasted_iota(jnp.int32, (size, width), 0).astype(jnp.float32) * freq
     cos_ref[...] = jnp.cos(angle)
@@ -106,6 +112,7 @@
         base_ref[stream, 1] = base_sin
         base_ref[stream, 2] = base_sin * sign
         base_ref[stream, 3] = base_cos * sign
+    loads[0].wait()
     lanes = lax.broadcasted_iota(jnp.int32, (8, half), 1)
     places = [chunks[stream] * size + half * stream + lanes for stream in range(2)]
 
@@ -121,7 +128,8 @@
     token = lax.broadcasted_iota(jnp.int32, (rows, half), 0) // per
     lane = lax.broadcasted_iota(jnp.int32, (rows, half), 1)
     pick[...] = jnp.where(token == lane, 1.0, 0.0).astype(jnp.bfloat16)
-    load.wait()
+    loads[1].wait()
+    loads[2].wait()
 
 
 def begin_kernel(half, factor, q_ref, pick, cos_ref, sin_ref, base_ref, start_ref, own0, own1,
@@ -158,20 +166,28 @@
                 for g in range(groups):
                     r = pl.ds(pl.multiple_of((2 * i + u) * TILE, TILE), TILE)
                     x = scores_of(qrot_ref[stream, g, r, :], pick[r, :], keys[g, :count, :])
-                    high = jnp.max(x, axis=1, keepdims=True)
-                    p = jnp.exp2((x - high) * factor).astype(jnp.bfloat16)
+                    p, high = weights_of(x, factor, None)
                     acc[g, r, :] = jnp.dot(p, values[g, :count, :], preferred_element_type=jnp.float32)
-                    top[g, r, :] = jnp.broadcast_to(high, (TILE, width))
+                    top[g, r, :] = high
             return carry
 
         lax.fori_loop(0, rows // (2 * TILE), body, 0)
+
+
+def weights_of(x, factor, before):
+    lanes = 128
+    pieces = [x[:, c:c + lanes] for c in range(0, x.shape[1], lanes)]
+    top = jnp.max(functools.reduce(jnp.maximum, pieces), axis=1, keepdims=True)
+    top = jnp.broadcast_to(top, pieces[0].shape)
+    if before is not None:
+        top = jnp.maximum(before, top)
+    p = jnp.concatenate([jnp.exp2((y - top) * factor).astype(jnp.bfloat16) for y in pieces], axis=1)
+    return p, top
 
 
 def update(factor, q, pick, k, v, acc, before):
     width = before.shape[-1]
-    x = scores_of(q, pick, k)
-    top = jnp.maximum(before, jnp.max(x, axis=1, keepdims=True))
-    p = jnp.exp2((x - top[:, :1]) * factor).astype(jnp.bfloat16)
+    p, top = weights_of(scores_of(q, pick, k), factor, before)
     scale = jnp.exp2((before - top) * factor)
     new = jnp.dot(p, v, preferred_element_type=jnp.float32)
     return acc[:, :width] * scale + new[:, :width], acc[:, width:] * scale + new[:, width:], top
@@ -179,7 +195,7 @@
 
 def middle_kernel(half, factor, stream, qrot_ref, pick, cos_ref, sin_ref, base_ref, start_ref, old_acc, old_top, pair_ref,
                   acc_ref, top_ref, keys, values):
-    core, chunks = my_chunks()
+    _, chunks = my_chunks()
     chunk = chunks[stream]
     size = 2 * half
     groups, rows, width = qrot_ref.shape[1:]
@@ -286,12 +302,16 @@
     def near(*values):
         return [pltpu.with_memory_space_constraint(x, pltpu.VMEM) for x in values]
 
+    def far(*values):
+        return [pltpu.with_memory_space_constraint(x, pltpu.HBM) for x in values]
+
     index = (jnp.arange(width, dtype=jnp.int32) % (width // 2)).astype(f32)
     freq = (ROPE_BASE ** (-(index * 2.0 / width)))[None, :]
     received = with_layout_constraint(to_sibling(key_value), Layout((0, 1, 2)))
-    q, *tables = pl.pallas_call(
+    kv, q, *tables = pl.pallas_call(
         functools.partial(tables_kernel, half),
         out_shape=(
+            local((rows, groups, pair), bf16),
             local((rows, heads, width), bf16),
             local((half * per, half), bf16),
             local((rows, width), f32),
@@ -299,14 +319,14 @@
             local((2, 4, 8, width), f32),
             local((2, 8, half), i32),
         ),
-        in_specs=[smem, vmem, hbm],
-        out_specs=(vmem,) * 6,
-        scratch_shapes=[pltpu.SemaphoreType.DMA(())],
+        in_specs=[vmem, hbm, hbm, hbm],
+        out_specs=(vmem,) * 7,
+        scratch_shapes=[pltpu.SMEM(doc_lengths.shape, i32), pltpu.SemaphoreType.DMA((3,))],
         cost_estimate=pl.CostEstimate(flops=10 ** 7, bytes_accessed=10 ** 6, transcendentals=10 ** 5),
         compiler_params=params,
         name="tables",
-    )(doc_lengths, *near(freq), queries)
-    received, q = lax.optimization_barrier((received, q))
+    )(*near(freq), *far(doc_lengths, key_value, queries))
+    received, kv, q = lax.optimization_barrier((received, kv, q))
     core = lax.rem(lax.axis_index("ctx"), 2)
     first = core * half
     second = (1 - core) * half
@@ -314,8 +334,8 @@
     def take(x, start):
         return lax.dynamic_slice_in_dim(x, start, half, 0)
 
-    own = jnp.concatenate([take(key_value, first), take(received, first)], 0).transpose(1, 0, 2)
-    own_other = jnp.concatenate([take(received, second), take(key_value, second)], 0).transpose(1, 0, 2)
+    own = jnp.concatenate([take(kv, first), take(received, first)], 0).transpose(1, 0, 2)
+    own_other = jnp.concatenate([take(received, second), take(kv, second)], 0).transpose(1, 0, 2)
 
     one = along_chain(own, 1)
     two = along_chain(own, 2)
@@ -353,7 +373,6 @@
             input_output_aliases={6: 0, 7: 1},
             cost_estimate=pl.CostEstimate(flops=10 ** 9, bytes_accessed=10 ** 6, transcendentals=10 ** 6),
             compiler_params=params,
-            name="middle%d" % stream,
         )(*near(*tables, acc, top, keys))
 
     acc0, top0 = middle(0, acc0, top0, near_pair)
@@ -372,7 +391,6 @@
             input_output_aliases={9: 0} if out else {},
             cost_estimate=pl.CostEstimate(flops=10 ** 9, bytes_accessed=10 ** 6, transcendentals=10 ** 6),
             compiler_params=params,
-            name="end%d" % stream,
         )(*near(*tables, acc, top, keys), *out)
 
     out = end(0, acc0, top0, far_pair)

time: 36.5 us -> 31.9 us (0.87)
  the two profiles are of different devices: /device:TPU:29 before, /device:TPU:23 now
where the time goes in v3:
time: 31.9 us; the launch traced here: 31.7 us
  Pallas kernels  16.2 us (51%)
  starting transfers between devices  11.3 us (35%)
  waiting for transfers between devices  3.84 us (12%)
    ppermute x3, starting transfers between devices, along_chain(): return lax.ppermute(value, 'ctx', pairs)  6.28 us
    pallas_call x1, Pallas kernels, shards(): pl.pallas_call(functools.partial(begin_kernel, half, factor), out_shape=(...  5.25 us
    ppermute x3, starting transfers between devices, to_sibling(): return lax.ppermute(value, 'ctx', [(i, i ^ 1) for i in range(count)])  5.02 us
    pallas_call x2, Pallas kernels, middle(): pl.pallas_call(functools.partial(middle_kernel, half, factor, stream), ou...  4.96 us
    pallas_call x2, Pallas kernels, end(): pl.pallas_call(functools.partial(end_kernel, half, factor, stream), out_s...  4.66 us
    ppermute x3, waiting for transfers between devices, along_chain(): return lax.ppermute(value, 'ctx', pairs)  3.83 us
    pallas_call x1, Pallas kernels, shards(): pl.pallas_call(functools.partial(tables_kernel, half), out_shape=(local((...  1.35 us
  transfers between devices with their start and end apart: 6, of which 2 were waited for; matrix products, arithmetic and copies ran while one was open for 0% of the time, Pallas kernels for 48%

profile of v3, /device:TPU:23, one launch (start us, length us, event | category | flops | bytes accessed | tf_op | source)
XLA Modules:
  0.0 31.7 jit_solution(13641616231980401798)
XLA Ops:
  0.0 0.7 %collective-permute-start = (bf16[256,2,256]{2,1,0:T(2,128)(2,1)}, bf16[256,2,256]{2,1,0:T(2,128)(2,1)S(1)}, u32[]{:S(2)}, u32[]{:S(2)}) collective-permute-start(bf16[256,2,256]{2,1,0:T(2,128)(2,1)} %kv_hbm.1), channel_id=1, source_target_pairs={{0,2},{2,0},{4,6},{6,4},{8,10},{10,8},{12,14},{14,12},{16,18},{18,... | collective-permute-start | bytes 786440 | tf_op jit(solution)/shard_map/ppermute | solution.py:33
  0.7 1.3 %tables.1 = (bf16[256,2,256]{2,1,0:T(2,128)(2,1)S(1)}, bf16[256,16,128]{2,1,0:T(8,128)(2,1)S(1)}, bf16[1024,128]{1,0:T(8,128)(2,1)S(1)}, f32[256,128]{1,0:T(8,12...) custom-call(f32[1,128]{1,0:T(1,128)S(1)} %fusion.3.freq_ref, s32[8]{0:T(128)} %docs_hbm.1, ...), custom_call_target="tpu_custom_call" | custom-call | flops 10000000 | bytes 1000000 | tf_op jit(solution)/shard_map/tables/pallas_call | solution.py:311
  2.0 0.0 collective-permute-done
  2.2 2.1 %collective-permute-start.2 = (bf16[2,256,256]{2,1,0:T(8,128)(2,1)S(1)}, bf16[2,256,256]{2,1,0:T(8,128)(2,1)S(1)}, u32[]{:S(2)}, u32[]{:S(2)}) collective-permute-start(bf16[2,256,256]{2,1,0:T(8,128)(2,1)S(1)} %maximum_bitcast_fusion.own0), channel_id=1, source_target_pairs={{0,8},{4,12},{8,16},{12,20},{16,24},{20,28},{24,30},{28,26},{30,22... | collective-permute-start | bytes 786440 | tf_op jit(solution)/shard_map/ppermute | solution.py:28
  4.3 2.1 %collective-permute-start.1 = (bf16[2,256,256]{2,1,0:T(8,128)(2,1)S(1)}, bf16[2,256,256]{2,1,0:T(8,128)(2,1)S(1)}, u32[]{:S(2)}, u32[]{:S(2)}) collective-permute-start(bf16[2,256,256]{2,1,0:T(8,128)(2,1)S(1)} %maximum_bitcast_fusion.own0), channel_id=1, source_target_pairs={{0,4},{4,8},{8,12},{12,16},{16,20},{20,24},{24,28},{28,30},{30,26}... | collective-permute-start | bytes 786440 | tf_op jit(solution)/shard_map/ppermute | solution.py:28
  6.5 5.2 %begin.1 = (bf16[2,2,1024,128]{3,2,1,0:T(8,128)(2,1)S(1)}, f32[2,1024,256]{2,1,0:T(8,128)S(1)}, f32[2,1024,128]{2,1,0:T(8,128)S(1)}, f32[2,1024,256]{2,1,0:T(8,128)S(1)}, f32[2,1024,128]{2,1,0:T(8,128)S(1)}) custom-call(bf16[256,16,128]{2,1,0:T(8,128)(2,1)S(1)} %get-tuple-element.32.q_ref, bf16[1024,128]{1,0:T(8,128)(2,1)S(1)} %get-tuple-element.33.pick, ...), custom_call_target="tpu_custom_call" | custom-call | flops 2000000000 | bytes 1000000 | tf_op jit(solution)/shard_map/begin/pallas_call | solution.py:345
  11.7 0.0 collective-permute-done.2
  11.7 0.7 %collective-permute-done.1 = bf16[2,256,256]{2,1,0:T(8,128)(2,1)S(1)} collective-permute-done((bf16[2,256,256]{2,1,0:T(8,128)(2,1)S(1)}, bf16[2,256,256]{2,1,0:T(8,128)(2,1)S(1)}, u32[]{:S(2)}, u32[]{:S(2)}) %collective-permute-start.1) | collective-permute-done | bytes 262176 | tf_op jit(solution)/shard_map/ppermute | solution.py:28
  12.4 0.1 pad_maximum_fusion.pair_ref
  12.5 3.5 %collective-permute-start.4 = (bf16[2,2,256,256]{3,2,1,0:T(8,128)(2,1)S(1)}, bf16[2,2,256,256]{3,2,1,0:T(8,128)(2,1)S(1)}, u32[]{:S(2)}, u32[]{:S(2)}) collective-permute-start(bf16[2,2,256,256]{3,2,1,0:T(8,128)(2,1)S(1)} %pad_maximum_fusion.pair_ref), channel_id=1, source_target_pairs={{0,2},{2,0},{4,6},{6,4},{8,10},{10,8},{12,14},{14,12},{16,18},{18,... | collective-permute-start | bytes 1572872 | tf_op jit(solution)/shard_map/ppermute | solution.py:33
  15.9 2.1 %collective-permute-start.3 = (bf16[2,2,256,256]{3,2,1,0:T(8,128)(2,1)S(1)}, bf16[2,2,256,256]{3,2,1,0:T(8,128)(2,1)S(1)}, u32[]{:S(2)}, u32[]{:S(2)}) collective-permute-start(bf16[2,2,256,256]{3,2,1,0:T(8,128)(2,1)S(1)} %pad_maximum_fusion.pair_ref), channel_id=1, source_target_pairs={{0,8},{4,12},{8,16},{12,20},{16,24},{20,28},{24,30},{28,26},{30,22... | collective-permute-start | bytes 1572872 | tf_op jit(solution)/shard_map/ppermute | solution.py:28
  18.0 2.8 %shard_map.37 = (f32[2,1024,256]{2,1,0:T(8,128)S(1)}, f32[2,1024,128]{2,1,0:T(8,128)S(1)}) custom-call(bf16[2,2,1024,128]{3,2,1,0:T(8,128)(2,1)S(1)} %get-tuple-element.40.qrot_ref, bf16[1024,128]{1,0:T(8,128)(2,1)S(1)} %get-tuple-element.33.pick, f32[256,128]{1,0:T(8,128)S(1)} %get-tuple-element.34.cos_ref, ...), custom_call_target="tpu_custom_call", output_to_operand_aliasing={{0}: (6, {}), {1}: (7, {})} | custom-call | flops 1000000000 | bytes 1000000 | tf_op jit(solution)/shard_map/pallas_call | solution.py:367
  20.8 0.0 collective-permute-done.4.pair_ref
  20.8 2.2 %shard_map.38 = (f32[2,1024,256]{2,1,0:T(8,128)S(1)}, f32[2,1024,128]{2,1,0:T(8,128)S(1)}) custom-call(bf16[2,2,1024,128]{3,2,1,0:T(8,128)(2,1)S(1)} %get-tuple-element.40.qrot_ref, bf16[1024,128]{1,0:T(8,128)(2,1)S(1)} %get-tuple-element.33.pick, f32[256,128]{1,0:T(8,128)S(1)} %get-tuple-element.34.cos_ref, ...), custom_call_target="tpu_custom_call", output_to_operand_aliasing={{0}: (6, {}), {1}: (7, {})} | custom-call | flops 1000000000 | bytes 1000000 | tf_op jit(solution)/shard_map/pallas_call | solution.py:367
  23.0 3.1 %collective-permute-done.3.pair_ref = bf16[2,2,256,256]{3,2,1,0:T(8,128)(2,1)S(1)} collective-permute-done((bf16[2,2,256,256]{3,2,1,0:T(8,128)(2,1)S(1)}, bf16[2,2,256,256]{3,2,1,0:T(8,128)(2,1)S(1)}, u32[]{:S(2)}, u32[]{:S(2)}) %collective-permute-start.3) | collective-permute-done | bytes 524320 | tf_op jit(solution)/shard_map/ppermute | solution.py:28
  26.1 0.9 %collective-permute-start.5 = (bf16[2,2,256,256]{3,2,1,0:T(8,128)(2,1)S(1)}, bf16[2,2,256,256]{3,2,1,0:T(8,128)(2,1)S(1)}, u32[]{:S(2)}, u32[]{:S(2)}) collective-permute-start(bf16[2,2,256,256]{3,2,1,0:T(8,128)(2,1)S(1)} %collective-permute-done.3.pair_ref), channel_id=1, source_target_pairs={{0,2},{2,0},{4,6},{6,4},{8,10},{10,8},{12,14},{14,12},{16,18},{18,... | collective-permute-start | bytes 1572872 | tf_op jit(solution)/shard_map/ppermute | solution.py:33
  27.0 3.6 %shard_map.39.refs_0_ = bf16[256,16,128]{2,1,0:T(8,128)(2,1)} custom-call(bf16[2,2,1024,128]{3,2,1,0:T(8,128)(2,1)S(1)} %get-tuple-element.40.qrot_ref, bf16[1024,128]{1,0:T(8,128)(2,1)S(1)} %get-tuple-element.33.pick, f32[256,128]{1,0:T(8,128)S(1)} %get-tuple-element.34.cos_ref, f32[256,128]{1,0:T(8,128)S(1)} %get-tuple-element.35.sin_ref, ...), custom_call_target="tpu_custom_call" | custom-call | flops 1000000000 | bytes 1000000 | tf_op jit(solution)/shard_map/pallas_call | solution.py:385
  30.6 0.0 collective-permute-done.5.pair_ref
  30.6 1.1 %shard_map.40 = bf16[256,16,128]{2,1,0:T(8,128)(2,1)} custom-call(bf16[2,2,1024,128]{3,2,1,0:T(8,128)(2,1)S(1)} %get-tuple-element.40.qrot_ref, bf16[1024,128]{1,0:T(8,128)(2,1)S(1)} %get-tuple-element.33.pick, f32[256,128]{1,0:T(8,128)S(1)} %get-tuple-element.34.cos_ref, f32[256,128]{1,0:T(8,128)S(1)} %get-tuple-element.35.sin_ref, ...), custom_call_target="tpu_custom_call", output_to_operand_aliasing={{}: (9, {})} | custom-call | flops 1000000000 | bytes 1000000 | tf_op jit(solution)/shard_map/pallas_call | solution.py:385
  (6 shorter events, 0.2 us)
Async XLA Ops:
  0.0 2.0 %collective-permute-start = (bf16[256,2,256]{2,1,0:T(2,128)(2,1)}, bf16[256,2,256]{2,1,0:T(2,128)(2,1)S(1)}, u32[]{:S(2)}, u32[]{:S(2)}) collective-permute-start(bf16[256,2,256]{2,1,0:T(2,128)(2,1)} %kv_hbm.1), channel_id=1, source_target_pairs={{0,2},{2,0},{4,6},{6,4},{8,10},{10,8},{12,14},{14,12},{16,18},{18,... | collective-permute-start | bytes 786440 | tf_op jit(solution)/shard_map/ppermute | solution.py:33
  2.2 9.5 %collective-permute-start.2 = (bf16[2,256,256]{2,1,0:T(8,128)(2,1)S(1)}, bf16[2,256,256]{2,1,0:T(8,128)(2,1)S(1)}, u32[]{:S(2)}, u32[]{:S(2)}) collective-permute-start(bf16[2,256,256]{2,1,0:T(8,128)(2,1)S(1)} %maximum_bitcast_fusion.own0), channel_id=1, source_target_pairs={{0,8},{4,12},{8,16},{12,20},{16,24},{20,28},{24,30},{28,26},{30,22... | collective-permute-start | bytes 786440 | tf_op jit(solution)/shard_map/ppermute | solution.py:28
  4.3 8.1 %collective-permute-start.1 = (bf16[2,256,256]{2,1,0:T(8,128)(2,1)S(1)}, bf16[2,256,256]{2,1,0:T(8,128)(2,1)S(1)}, u32[]{:S(2)}, u32[]{:S(2)}) collective-permute-start(bf16[2,256,256]{2,1,0:T(8,128)(2,1)S(1)} %maximum_bitcast_fusion.own0), channel_id=1, source_target_pairs={{0,4},{4,8},{8,12},{12,16},{16,20},{20,24},{24,28},{28,30},{30,26}... | collective-permute-start | bytes 786440 | tf_op jit(solution)/shard_map/ppermute | solution.py:28
  12.5 8.3 %collective-permute-start.4 = (bf16[2,2,256,256]{3,2,1,0:T(8,128)(2,1)S(1)}, bf16[2,2,256,256]{3,2,1,0:T(8,128)(2,1)S(1)}, u32[]{:S(2)}, u32[]{:S(2)}) collective-permute-start(bf16[2,2,256,256]{3,2,1,0:T(8,128)(2,1)S(1)} %pad_maximum_fusion.pair_ref), channel_id=1, source_target_pairs={{0,2},{2,0},{4,6},{6,4},{8,10},{10,8},{12,14},{14,12},{16,18},{18,... | collective-permute-start | bytes 1572872 | tf_op jit(solution)/shard_map/ppermute | solution.py:33
  15.9 10.2 %collective-permute-start.3 = (bf16[2,2,256,256]{3,2,1,0:T(8,128)(2,1)S(1)}, bf16[2,2,256,256]{3,2,1,0:T(8,128)(2,1)S(1)}, u32[]{:S(2)}, u32[]{:S(2)}) collective-permute-start(bf16[2,2,256,256]{3,2,1,0:T(8,128)(2,1)S(1)} %pad_maximum_fusion.pair_ref), channel_id=1, source_target_pairs={{0,8},{4,12},{8,16},{12,20},{16,24},{20,28},{24,30},{28,26},{30,22... | collective-permute-start | bytes 1572872 | tf_op jit(solution)/shard_map/ppermute | solution.py:28
  26.1 4.5 %collective-permute-start.5 = (bf16[2,2,256,256]{3,2,1,0:T(8,128)(2,1)S(1)}, bf16[2,2,256,256]{3,2,1,0:T(8,128)(2,1)S(1)}, u32[]{:S(2)}, u32[]{:S(2)}) collective-permute-start(bf16[2,2,256,256]{3,2,1,0:T(8,128)(2,1)S(1)} %collective-permute-done.3.pair_ref), channel_id=1, source_target_pairs={{0,2},{2,0},{4,6},{6,4},{8,10},{10,8},{12,14},{14,12},{16,18},{18,... | collective-permute-start | bytes 1572872 | tf_op jit(solution)/shard_map/ppermute | solution.py:33

commit v4 on v3

--- a/solution.py
+++ b/solution.py
@@ -52,30 +52,40 @@
     return pltpu.roll(x, x.shape[-1] // 2, axis=x.ndim - 1)
 
 
-def load_keys(chunk_ref, first, count, tables, stream, step, chunk, causal, keys, values, at):
-    cos_ref, sin_ref, base_ref, start_ref = tables
-    size, width = cos_ref.shape
-    half = start_ref.shape[-1]
-    c = cos_ref[pl.ds(first, count), :]
-    s = sin_ref[pl.ds(first, count), :]
+def chunk_rotation(tables, stream, step):
+    cos_ref, sin_ref, base_ref, _ = tables
+    c = cos_ref[...]
+    s = sin_ref[...]
     cosine = base_ref[stream, 0, step:step + 1, :] * c - base_ref[stream, 1, step:step + 1, :] * s
     sine = base_ref[stream, 2, step:step + 1, :] * c + base_ref[stream, 3, step:step + 1, :] * s
+    return cosine, sine
+
+
+def rotate_keys(chunk_ref, g, rotation):
+    cosine, sine = rotation
+    k = chunk_ref[g, :, :cosine.shape[-1]].astype(jnp.float32)
+    return (k * cosine + swap_halves(k) * sine).astype(jnp.bfloat16)
+
+
+def hide(start_ref, stream, step, chunk, first, count, causal, hidden, at):
+    half = start_ref.shape[-1]
+    size = 2 * half
     offset = lax.broadcasted_iota(jnp.int32, (count, half), 0)
     visible = offset >= start_ref[stream, 0:1, :] - ((chunk - step) * size + first)
     if causal:
         query = lax.broadcasted_iota(jnp.int32, (count, half), 1) + half * stream
         visible = visible & (offset + first <= query)
-    hidden = jnp.where(visible, 0.0, HIDDEN).astype(jnp.bfloat16)
-    for g in range(keys.shape[0]):
-        k = chunk_ref[g, pl.ds(first, count), :width].astype(jnp.float32)
-        keys[g, pl.ds(at, count), :width] = (k * cosine + swap_halves(k) * sine).astype(jnp.bfloat16)
-        keys[g, pl.ds(at, count), width:] = hidden
-        values[g, pl.ds(at, count), :width] = chunk_ref[g, pl.ds(first, count), width:]
-
-
-def fill_ones(values):
-    width = values.shape[-1] // 2
-    values[:, :, width:] = jnp.ones(values.shape[:2] + (width,), jnp.bfloat16)
+    hidden[pl.ds(at, count), :] = jnp.where(visible, 0.0, HIDDEN).astype(jnp.bfloat16)
+
+
+def masked_keys(pieces, hidden):
+    k = jnp.concatenate(pieces, axis=0)
+    return jnp.concatenate([k, hidden[:k.shape[0], :]], axis=1)
+
+
+def counted_values(pieces):
+    v = jnp.concatenate(pieces, axis=0)
+    return jnp.concatenate([v, jnp.ones_like(v)], axis=1)
 
 
 def scores_of(q, pick, k):
@@ -132,46 +142,58 @@
     loads[2].wait()
 
 
-def begin_kernel(half, factor, q_ref, pick, cos_ref, sin_ref, base_ref, start_ref, own0, own1,
-                 qrot_ref, acc0, top0, acc1, top1, work, keys, values):
+def rotate_kernel(chunk_ref, cos_ref, sin_ref, base_ref, out_ref):
+    width = cos_ref.shape[-1]
+    rotation = chunk_rotation((cos_ref, sin_ref, base_ref, None), 0, 0)
+    for g in range(chunk_ref.shape[0]):
+        out_ref[g, :, :width] = rotate_keys(chunk_ref, g, rotation)
+        out_ref[g, :, width:] = chunk_ref[g, :, width:]
+
+
+def begin_kernel(half, factor, stream, q_ref, pick, cos_ref, sin_ref, base_ref, start_ref, own,
+                 qrot_ref, acc, top, work, keys, hidden):
     core, chunks = my_chunks()
-    groups, rows, width = qrot_ref.shape[1:]
+    groups, rows, width = qrot_ref.shape
     per = rows // half
-    fill_ones(values)
     tables = (cos_ref, sin_ref, base_ref, start_ref)
     tokens = 16
-    for stream, own, acc, top in ((0, own0, acc0, top0), (1, own1, acc1, top1)):
-        c = cos_ref[pl.ds(half * stream, half), :]
-        s = sin_ref[pl.ds(half * stream, half), :]
-        work[0] = (base_ref[stream, 0, 0:1, :] * c - base_ref[stream, 1, 0:1, :] * s)[:, None, :]
-        work[1] = (base_ref[stream, 2, 0:1, :] * c + base_ref[stream, 3, 0:1, :] * s)[:, None, :]
-        count = half * (1 + stream)
-        load_keys(own, 0, count, tables, stream, 0, chunks[stream], True, keys, values, 0)
-        base_row = first_row(core, stream, half)
-
-        def rope_step(i, carry):
-            at = i * tokens
-            x = q_ref[pl.ds(base_row + at, tokens)].astype(jnp.float32)
-            y = x * work[0, pl.ds(at, tokens)] + swap_halves(x) * work[1, pl.ds(at, tokens)]
+    c = cos_ref[pl.ds(half * stream, half), :]
+    s = sin_ref[pl.ds(half * stream, half), :]
+    work[0] = (base_ref[stream, 0, 0:1, :] * c - base_ref[stream, 1, 0:1, :] * s)[:, None, :]
+    work[1] = (base_ref[stream, 2, 0:1, :] * c + base_ref[stream, 3, 0:1, :] * s)[:, None, :]
+    count = half * (1 + stream)
+    hide(start_ref, stream, 0, chunks[stream], 0, count, True, hidden, 0)
+    if stream == 1:
+        rotation = chunk_rotation(tables, 1, 0)
+        for g in range(groups):
+            keys[g] = rotate_keys(own, g, rotation)
+    base_row = first_row(core, stream, half)
+
+    def rope_step(i, carry):
+        at = i * tokens
+        x = q_ref[pl.ds(base_row + at, tokens)].astype(jnp.float32)
+        y = x * work[0, pl.ds(at, tokens)] + swap_halves(x) * work[1, pl.ds(at, tokens)]
+        for g in range(groups):
+            piece = y[:, g * per:(g + 1) * per, :].reshape(tokens * per, width)
+            r = pl.ds(pl.multiple_of(at * per, tokens * per), tokens * per)
+            qrot_ref[g, r, :] = piece.astype(jnp.bfloat16)
+        return carry
+
+    lax.fori_loop(0, half // tokens, rope_step, 0)
+
+    def body(i, carry):
+        for u in range(2):
             for g in range(groups):
-                piece = y[:, g * per:(g + 1) * per, :].reshape(tokens * per, width)
-                r = pl.ds(pl.multiple_of(at * per, tokens * per), tokens * per)
-                qrot_ref[stream, g, r, :] = piece.astype(jnp.bfloat16)
-            return carry
-
-        lax.fori_loop(0, half // tokens, rope_step, 0)
-
-        def body(i, carry):
-            for u in range(2):
-                for g in range(groups):
-                    r = pl.ds(pl.multiple_of((2 * i + u) * TILE, TILE), TILE)
-                    x = scores_of(qrot_ref[stream, g, r, :], pick[r, :], keys[g, :count, :])
-                    p, high = weights_of(x, factor, None)
-                    acc[g, r, :] = jnp.dot(p, values[g, :count, :], preferred_element_type=jnp.float32)
-                    top[g, r, :] = high
-            return carry
-
-        lax.fori_loop(0, rows // (2 * TILE), body, 0)
+                r = pl.ds(pl.multiple_of((2 * i + u) * TILE, TILE), TILE)
+                k = keys[g] if stream == 1 else own[g, :count, :width]
+                x = scores_of(qrot_ref[g, r, :], pick[r, :], masked_keys([k], hidden))
+                p, high = weights_of(x, factor, None)
+                v = counted_values([own[g, :count, width:]])
+                acc[g, r, :] = jnp.dot(p, v, preferred_element_type=jnp.float32)
+                top[g, r, :] = high
+        return carry
+
+    lax.fori_loop(0, rows // (2 * TILE), body, 0)
 
 
 def weights_of(x, factor, before):
@@ -193,51 +215,64 @@
     return acc[:, :width] * scale + new[:, :width], acc[:, width:] * scale + new[:, width:], top
 
 
+def seeing(start_ref, stream, place, iterations):
+    starts = start_ref[stream]
+    span = starts.shape[-1] // iterations
+    lane = lax.broadcasted_iota(jnp.int32, starts.shape, 1)
+    reached = jnp.where((starts < place) & (lane % span == 0), 1, 0)
+    return lax.div(jnp.sum(reached), starts.shape[0])
+
+
 def middle_kernel(half, factor, stream, qrot_ref, pick, cos_ref, sin_ref, base_ref, start_ref, old_acc, old_top, pair_ref,
-                  acc_ref, top_ref, keys, values):
+                  acc_ref, top_ref, hidden):
     _, chunks = my_chunks()
     chunk = chunks[stream]
     size = 2 * half
-    groups, rows, width = qrot_ref.shape[1:]
-    tables = (cos_ref, sin_ref, base_ref, start_ref)
-    earliest = jnp.min(start_ref[stream])
-
-    def work(chunks_used):
-        fill_ones(values)
-        for n in range(chunks_used):
-            load_keys(pair_ref.at[n], 0, size, tables, stream, 1 + n, chunk, False, keys, values, n * size)
-        count = chunks_used * size
+    groups, rows, width = qrot_ref.shape
+    iterations = rows // (2 * TILE)
+
+    def work(chunks_used, low, high):
+        def piece(g, lanes):
+            return [pair_ref[n, g, :, lanes] for n in range(chunks_used)]
 
         def body(i, carry):
             for u in range(2):
                 for g in range(groups):
                     r = pl.ds(pl.multiple_of((2 * i + u) * TILE, TILE), TILE)
                     first, second, top = update(
-                        factor, qrot_ref[stream, g, r, :], pick[r, :], keys[g, :count, :], values[g, :count, :],
-                        old_acc[g, r, :], old_top[g, r, :])
+                        factor, qrot_ref[g, r, :], pick[r, :], masked_keys(piece(g, slice(0, width)), hidden),
+                        counted_values(piece(g, slice(width, None))), old_acc[g, r, :], old_top[g, r, :])
                     acc_ref[g, r, :width] = first
                     acc_ref[g, r, width:] = second
                     top_ref[g, r, :] = top
             return carry
 
-        lax.fori_loop(0, rows // (2 * TILE), body, 0)
-
-    far = earliest < (chunk - 1) * size
-    close = earliest < chunk * size
-    pl.when(far)(lambda: work(2))
-    pl.when(close & jnp.logical_not(far))(lambda: work(1))
+        lax.fori_loop(low, high, body, 0)
+
+    close = seeing(start_ref, stream, chunk * size, iterations)
+    far = seeing(start_ref, stream, (chunk - 1) * size, iterations)
+
+    @pl.when(close > 0)
+    def _():
+        hide(start_ref, stream, 1, chunk, 0, size, False, hidden, 0)
+
+        @pl.when(far > 0)
+        def _():
+            hide(start_ref, stream, 2, chunk, 0, size, False, hidden, size)
+            work(2, 0, far)
+
+        work(1, far, close)
 
 
 def end_kernel(half, factor, stream, qrot_ref, pick, cos_ref, sin_ref, base_ref, start_ref, acc_ref, top_ref, pair_ref, *refs):
-    out_hbm, keys, values, result, sent = refs[-5:]
+    out_hbm, hidden, result, sent = refs[-4:]
     core, chunks = my_chunks()
     chunk = chunks[stream]
     size = 2 * half
-    groups, rows, width = qrot_ref.shape[1:]
+    groups, rows, width = qrot_ref.shape
     per = rows // half
     tokens = TILE // per
-    tables = (cos_ref, sin_ref, base_ref, start_ref)
-    earliest = jnp.min(start_ref[stream])
+    iterations = rows // (2 * TILE)
     base_row = first_row(core, stream, half)
 
     def send(part):
@@ -245,7 +280,7 @@
         return pltpu.make_async_copy(
             result.at[pl.ds(part * span, span)], out_hbm.at[pl.ds(base_row + part * span, span)], sent.at[part])
 
-    def finish(one):
+    def finish(one, low, high):
         def body(i, carry):
             for u in range(2):
                 at = 2 * i + u
@@ -258,29 +293,37 @@
             send(i).start()
             return carry
 
-        lax.fori_loop(0, rows // (2 * TILE), body, 0)
-
-    def work(chunks_used):
-        fill_ones(values)
-        used = 0
-        for n in range(chunks_used):
-            begin = half * stream if n == 1 else 0
-            load_keys(pair_ref.at[n], begin, size - begin, tables, stream, 3 + n, chunk, False, keys, values, used)
-            used += size - begin
+        lax.fori_loop(low, high, body, 0)
+
+    begin = half * stream
+
+    def work(spans, low, high):
+        def piece(g, lanes):
+            return [pair_ref[n, g, span, lanes] for n, span in enumerate(spans)]
 
         def one(g, r):
             first, second, _ = update(
-                factor, qrot_ref[stream, g, r, :], pick[r, :], keys[g, :used, :], values[g, :used, :],
-                acc_ref[g, r, :], top_ref[g, r, :])
+                factor, qrot_ref[g, r, :], pick[r, :], masked_keys(piece(g, slice(0, width)), hidden),
+                counted_values(piece(g, slice(width, None))), acc_ref[g, r, :], top_ref[g, r, :])
             return first, second
 
-        finish(one)
-
-    far = earliest < (chunk - 3) * size
-    close = earliest < (chunk - 2) * size
-    pl.when(far)(lambda: work(2))
-    pl.when(close & jnp.logical_not(far))(lambda: work(1))
-    pl.when(jnp.logical_not(close))(lambda: finish(lambda g, r: (acc_ref[g, r, :width], acc_ref[g, r, width:])))
+        finish(one, low, high)
+
+    close = seeing(start_ref, stream, (chunk - 2) * size, iterations)
+    far = seeing(start_ref, stream, (chunk - 3) * size, iterations)
+
+    @pl.when(close > 0)
+    def _():
+        hide(start_ref, stream, 3, chunk, 0, size, False, hidden, 0)
+
+        @pl.when(far > 0)
+        def _():
+            hide(start_ref, stream, 4, chunk, begin, size - begin, False, hidden, size)
+            work((slice(0, size), slice(begin, size)), 0, far)
+
+        work((slice(0, size),), far, close)
+
+    finish(lambda g, r: (acc_ref[g, r, :width], acc_ref[g, r, width:]), close, iterations)
     send(0).wait()
     send(1).wait()
 
@@ -337,33 +380,44 @@
     own = jnp.concatenate([take(kv, first), take(received, first)], 0).transpose(1, 0, 2)
     own_other = jnp.concatenate([take(received, second), take(kv, second)], 0).transpose(1, 0, 2)
 
+    own = pl.pallas_call(
+        rotate_kernel,
+        out_shape=local((groups, rows, pair), bf16),
+        in_specs=[vmem] * 4,
+        out_specs=vmem,
+        cost_estimate=pl.CostEstimate(flops=10 ** 6, bytes_accessed=10 ** 6, transcendentals=0),
+        compiler_params=params,
+        name="rotate",
+    )(*near(own, *tables[1:4]))
+
     one = along_chain(own, 1)
     two = along_chain(own, 2)
 
     state = (local((groups, half * per, 2 * width), f32), local((groups, half * per, width), f32))
-    key_scratch = [pltpu.VMEM((groups, 2 * rows, 2 * width), bf16), pltpu.VMEM((groups, 2 * rows, 2 * width), bf16)]
-    qrot, acc0, top0, acc1, top1 = pl.pallas_call(
-        functools.partial(begin_kernel, half, factor),
-        out_shape=(local((2, groups, half * per, width), bf16),) + state + state,
-        in_specs=[vmem] * 8,
-        out_specs=(vmem,) * 5,
-        scratch_shapes=[
-            pltpu.VMEM((2, half, 1, width), f32),
-            pltpu.VMEM((groups, rows, 2 * width), bf16),
-            pltpu.VMEM((groups, rows, 2 * width), bf16),
-        ],
-        cost_estimate=pl.CostEstimate(flops=2 * 10 ** 9, bytes_accessed=10 ** 6, transcendentals=10 ** 6),
-        compiler_params=params,
-        name="begin",
-    )(*near(q, *tables, own, own_other))
-    tables = [qrot] + tables
-
+    key_scratch = [pltpu.VMEM((2 * rows, half), bf16)]
+
+    def begin(stream, own_keys):
+        return pl.pallas_call(
+            functools.partial(begin_kernel, half, factor, stream),
+            out_shape=(local((groups, half * per, width), bf16),) + state,
+            in_specs=[vmem] * 7,
+            out_specs=(vmem,) * 3,
+            scratch_shapes=[
+                pltpu.VMEM((2, half, 1, width), f32),
+                pltpu.VMEM((groups, rows, width), bf16),
+                pltpu.VMEM((rows, half), bf16),
+            ],
+            cost_estimate=pl.CostEstimate(flops=10 ** 9, bytes_accessed=10 ** 6, transcendentals=10 ** 6),
+            compiler_params=params,
+        )(*near(q, *tables, own_keys))
+
+    qrot0, acc0, top0 = begin(0, own)
+    qrot1, acc1, top1 = begin(1, own_other)
     near_pair = jnp.stack([one, two])
     near_pair, acc0, acc1 = lax.optimization_barrier((near_pair, acc0, acc1))
     far_pair = along_chain(near_pair, 2)
-    near_other = to_sibling(near_pair)
-
-    def middle(stream, acc, top, keys):
+
+    def middle(stream, qrot, acc, top, keys):
         return pl.pallas_call(
             functools.partial(middle_kernel, half, factor, stream),
             out_shape=state,
@@ -373,15 +427,17 @@
             input_output_aliases={6: 0, 7: 1},
             cost_estimate=pl.CostEstimate(flops=10 ** 9, bytes_accessed=10 ** 6, transcendentals=10 ** 6),
             compiler_params=params,
-        )(*near(*tables, acc, top, keys))
-
-    acc0, top0 = middle(0, acc0, top0, near_pair)
-    acc1, top1 = middle(1, acc1, top1, near_other)
+        )(*near(qrot, *tables, acc, top, keys))
+
+    acc0, top0 = middle(0, qrot0, acc0, top0, near_pair)
+    near_pair, acc0 = lax.optimization_barrier((near_pair, acc0))
+    near_other = to_sibling(near_pair)
+    acc1, top1 = middle(1, qrot1, acc1, top1, near_other)
 
     far_pair, acc0, acc1 = lax.optimization_barrier((far_pair, acc0, acc1))
     far_other = to_sibling(far_pair)
 
-    def end(stream, acc, top, keys, *out):
+    def end(stream, qrot, acc, top, keys, *out):
         return pl.pallas_call(
             functools.partial(end_kernel, half, factor, stream),
             out_shape=pltpu.HBM((rows, heads, width), bf16),
@@ -391,10 +447,10 @@
             input_output_aliases={9: 0} if out else {},
             cost_estimate=pl.CostEstimate(flops=10 ** 9, bytes_accessed=10 ** 6, transcendentals=10 ** 6),
             compiler_params=params,
-        )(*near(*tables, acc, top, keys), *out)
-
-    out = end(0, acc0, top0, far_pair)
-    return end(1, acc1, top1, far_other, out)
+        )(*near(qrot, *tables, acc, top, keys), *out)
+
+    out = end(0, qrot0, acc0, top0, far_pair)
+    return end(1, qrot1, acc1, top1, far_other, out)
 
 
 def solution(mesh):

time: 31.9 us -> 33.9 us (1.063)
  the two profiles are of different devices: /device:TPU:23 before, /device:TPU:26 now
where the time goes in v4:
time: 33.9 us; the launch traced here: 33.7 us
  Pallas kernels  15.2 us (45%)
  waiting for transfers between devices  9.6 us (28%)
  starting transfers between devices  8.57 us (25%)
    ppermute x3, waiting for transfers between devices, along_chain(): return lax.ppermute(value, 'ctx', pairs)  8.34 us
    ppermute x3, starting transfers between devices, along_chain(): return lax.ppermute(value, 'ctx', pairs)  7.5 us
    pallas_call x2, Pallas kernels, begin(): pl.pallas_call(functools.partial(begin_kernel, half, factor, stream), out...  5.15 us
    pallas_call x2, Pallas kernels, middle(): pl.pallas_call(functools.partial(middle_kernel, half, factor, stream), ou...  4.85 us
    pallas_call x2, Pallas kernels, end(): pl.pallas_call(functools.partial(end_kernel, half, factor, stream), out_s...  3.7 us
    pallas_call x1, Pallas kernels, shards(): pl.pallas_call(functools.partial(tables_kernel, half), out_shape=(local((...  1.35 us
    ppermute x3, waiting for transfers between devices, to_sibling(): return lax.ppermute(value, 'ctx', [(i, i ^ 1) for i in range(count)])  1.26 us
    ppermute x3, starting transfers between devices, to_sibling(): return lax.ppermute(value, 'ctx', [(i, i ^ 1) for i in range(count)])  1.07 us
  transfers between devices with their start and end apart: 6, of which 4 were waited for; matrix products, arithmetic and copies ran while one was open for 0% of the time, Pallas kernels for 30%

profile of v4, /device:TPU:26, one launch (start us, length us, event | category | flops | bytes accessed | tf_op | source)
XLA Modules:
  0.0 33.7 jit_solution(16697134271704056237)
XLA Ops:
  0.0 0.0 collective-permute-start
  0.0 1.3 %tables.1 = (bf16[256,2,256]{2,1,0:T(2,128)(2,1)S(1)}, bf16[256,16,128]{2,1,0:T(8,128)(2,1)S(1)}, bf16[1024,128]{1,0:T(8,128)(2,1)S(1)}, f32[256,128]{1,0:T(8,12...) custom-call(f32[1,128]{1,0:T(1,128)S(1)} %fusion.3.freq_ref, s32[8]{0:T(128)} %docs_hbm.1, ...), custom_call_target="tpu_custom_call" | custom-call | flops 10000000 | bytes 1000000 | tf_op jit(solution)/shard_map/tables/pallas_call | solution.py:354
  1.4 0.4 %collective-permute-done = bf16[256,2,256]{2,1,0:T(2,128)(2,1)S(1)} collective-permute-done((bf16[256,2,256]{2,1,0:T(2,128)(2,1)}, bf16[256,2,256]{2,1,0:T(2,128)(2,1)S(1)}, u32[]{:S(2)}, u32[]{:S(2)}) %collective-permute-start) | collective-permute-done | bytes 262176 | tf_op jit(solution)/shard_map/ppermute | solution.py:33
  1.9 0.1 rotate.1.own
  2.0 3.2 %collective-permute-start.2 = (bf16[2,256,256]{2,1,0:T(8,128)(2,1)S(1)}, bf16[2,256,256]{2,1,0:T(8,128)(2,1)S(1)}, u32[]{:S(2)}, u32[]{:S(2)}) collective-permute-start(bf16[2,256,256]{2,1,0:T(8,128)(2,1)S(1)} %rotate.1.own), channel_id=1, source_target_pairs={{0,8},{4,12},{8,16},{12,20},{16,24},{20,28},{24,30},{28,26},{30,22... | collective-permute-start | bytes 786440 | tf_op jit(solution)/shard_map/ppermute | solution.py:28
  5.2 2.4 %collective-permute-start.1 = (bf16[2,256,256]{2,1,0:T(8,128)(2,1)S(1)}, bf16[2,256,256]{2,1,0:T(8,128)(2,1)S(1)}, u32[]{:S(2)}, u32[]{:S(2)}) collective-permute-start(bf16[2,256,256]{2,1,0:T(8,128)(2,1)S(1)} %rotate.1.own), channel_id=1, source_target_pairs={{0,4},{4,8},{8,12},{12,16},{16,20},{20,24},{24,28},{28,30},{30,26}... | collective-permute-start | bytes 786440 | tf_op jit(solution)/shard_map/ppermute | solution.py:28
  7.6 2.5 %shard_map.38 = (bf16[2,1024,128]{2,1,0:T(8,128)(2,1)S(1)}, f32[2,1024,256]{2,1,0:T(8,128)S(1)}, f32[2,1024,128]{2,1,0:T(8,128)S(1)}) custom-call(bf16[256,16,128]{2,1,0:T(8,128)(2,1)S(1)} %get-tuple-element.35.q_ref, bf16[1024,128]{1,0:T(8,128)(2,1)S(1)} %get-tuple-element.36.pick, f32[256,128]{1,0:T(8,128)S(1)} %get-tuple-element.37.cos_ref, ...), custom_call_target="tpu_custom_call" | custom-call | flops 1000000000 | bytes 1000000 | tf_op jit(solution)/shard_map/pallas_call | solution.py:400
  10.1 2.7 %shard_map.37 = (bf16[2,1024,128]{2,1,0:T(8,128)(2,1)S(1)}, f32[2,1024,256]{2,1,0:T(8,128)S(1)}, f32[2,1024,128]{2,1,0:T(8,128)S(1)}) custom-call(bf16[256,16,128]{2,1,0:T(8,128)(2,1)S(1)} %get-tuple-element.35.q_ref, bf16[1024,128]{1,0:T(8,128)(2,1)S(1)} %get-tuple-element.36.pick, f32[256,128]{1,0:T(8,128)S(1)} %get-tuple-element.37.cos_ref, ...), custom_call_target="tpu_custom_call" | custom-call | flops 1000000000 | bytes 1000000 | tf_op jit(solution)/shard_map/pallas_call | solution.py:400
  12.8 0.0 collective-permute-done.2
  12.8 1.6 %collective-permute-done.1 = bf16[2,256,256]{2,1,0:T(8,128)(2,1)S(1)} collective-permute-done((bf16[2,256,256]{2,1,0:T(8,128)(2,1)S(1)}, bf16[2,256,256]{2,1,0:T(8,128)(2,1)S(1)}, u32[]{:S(2)}, u32[]{:S(2)}) %collective-permute-start.1) | collective-permute-done | bytes 262176 | tf_op jit(solution)/shard_map/ppermute | solution.py:28
  14.5 0.1 pad_maximum_fusion.pair_ref
  14.5 2.4 %shard_map.39 = (f32[2,1024,256]{2,1,0:T(8,128)S(1)}, f32[2,1024,128]{2,1,0:T(8,128)S(1)}) custom-call(bf16[2,1024,128]{2,1,0:T(8,128)(2,1)S(1)} %get-tuple-element.47.qrot_ref, bf16[1024,128]{1,0:T(8,128)(2,1)S(1)} %get-tuple-element.36.pick, f32[256,128]{1,0:T(8,128)S(1)} %get-tuple-element.37.cos_ref, ...), custom_call_target="tpu_custom_call", output_to_operand_aliasing={{0}: (6, {}), {1}: (7, {})} | custom-call | flops 1000000000 | bytes 1000000 | tf_op jit(solution)/shard_map/pallas_call | solution.py:421
  17.0 1.1 %collective-permute-start.4 = (bf16[2,2,256,256]{3,2,1,0:T(8,128)(2,1)S(1)}, bf16[2,2,256,256]{3,2,1,0:T(8,128)(2,1)S(1)}, u32[]{:S(2)}, u32[]{:S(2)}) collective-permute-start(bf16[2,2,256,256]{3,2,1,0:T(8,128)(2,1)S(1)} %pad_maximum_fusion.pair_ref), channel_id=1, source_target_pairs={{0,2},{2,0},{4,6},{6,4},{8,10},{10,8},{12,14},{14,12},{16,18},{18,... | collective-permute-start | bytes 1572872 | tf_op jit(solution)/shard_map/ppermute | solution.py:33
  18.0 1.9 %collective-permute-start.3 = (bf16[2,2,256,256]{3,2,1,0:T(8,128)(2,1)S(1)}, bf16[2,2,256,256]{3,2,1,0:T(8,128)(2,1)S(1)}, u32[]{:S(2)}, u32[]{:S(2)}) collective-permute-start(bf16[2,2,256,256]{3,2,1,0:T(8,128)(2,1)S(1)} %pad_maximum_fusion.pair_ref), channel_id=1, source_target_pairs={{0,8},{4,12},{8,16},{12,20},{16,24},{20,28},{24,30},{28,26},{30,22... | collective-permute-start | bytes 1572872 | tf_op jit(solution)/shard_map/ppermute | solution.py:28
  19.9 0.0 collective-permute-done.4.pair_ref
  20.0 2.4 %shard_map.40 = (f32[2,1024,256]{2,1,0:T(8,128)S(1)}, f32[2,1024,128]{2,1,0:T(8,128)S(1)}) custom-call(bf16[2,1024,128]{2,1,0:T(8,128)(2,1)S(1)} %get-tuple-element.43.qrot_ref, bf16[1024,128]{1,0:T(8,128)(2,1)S(1)} %get-tuple-element.36.pick, f32[256,128]{1,0:T(8,128)S(1)} %get-tuple-element.37.cos_ref, ...), custom_call_target="tpu_custom_call", output_to_operand_aliasing={{0}: (6, {}), {1}: (7, {})} | custom-call | flops 1000000000 | bytes 1000000 | tf_op jit(solution)/shard_map/pallas_call | solution.py:421
  22.4 6.7 %collective-permute-done.3.pair_ref = bf16[2,2,256,256]{3,2,1,0:T(8,128)(2,1)S(1)} collective-permute-done((bf16[2,2,256,256]{3,2,1,0:T(8,128)(2,1)S(1)}, bf16[2,2,256,256]{3,2,1,0:T(8,128)(2,1)S(1)}, u32[]{:S(2)}, u32[]{:S(2)}) %collective-permute-start.3) | collective-permute-done | bytes 524320 | tf_op jit(solution)/shard_map/ppermute | solution.py:28
  29.1 0.0 collective-permute-start.5
  29.1 1.0 %shard_map.41.refs_0_ = bf16[256,16,128]{2,1,0:T(8,128)(2,1)} custom-call(bf16[2,1024,128]{2,1,0:T(8,128)(2,1)S(1)} %get-tuple-element.47.qrot_ref, bf16[1024,128]{1,0:T(8,128)(2,1)S(1)} %get-tuple-element.36.pick, f32[256,128]{1,0:T(8,128)S(1)} %get-tuple-element.37.cos_ref, f32[256,128]{1,0:T(8,128)S(1)} %get-tuple-element.38.sin_ref, ...), custom_call_target="tpu_custom_call" | custom-call | flops 1000000000 | bytes 1000000 | tf_op jit(solution)/shard_map/pallas_call | solution.py:441
  30.1 0.9 %collective-permute-done.5.pair_ref = bf16[2,2,256,256]{3,2,1,0:T(8,128)(2,1)S(1)} collective-permute-done((bf16[2,2,256,256]{3,2,1,0:T(8,128)(2,1)S(1)}, bf16[2,2,256,256]{3,2,1,0:T(8,128)(2,1)S(1)}, u32[]{:S(2)}, u32[]{:S(2)}) %collective-permute-start.5) | collective-permute-done | bytes 524320 | tf_op jit(solution)/shard_map/ppermute | solution.py:33
  31.0 2.7 %shard_map.42 = bf16[256,16,128]{2,1,0:T(8,128)(2,1)} custom-call(bf16[2,1024,128]{2,1,0:T(8,128)(2,1)S(1)} %get-tuple-element.43.qrot_ref, bf16[1024,128]{1,0:T(8,128)(2,1)S(1)} %get-tuple-element.36.pick, f32[256,128]{1,0:T(8,128)S(1)} %get-tuple-element.37.cos_ref, f32[256,128]{1,0:T(8,128)S(1)} %get-tuple-element.38.sin_ref, ...), custom_call_target="tpu_custom_call", output_to_operand_aliasing={{}: (9, {})} | custom-call | flops 1000000000 | bytes 1000000 | tf_op jit(solution)/shard_map/pallas_call | solution.py:441
  (6 shorter events, 0.2 us)
Async XLA Ops:
  0.0 1.7 %collective-permute-start = (bf16[256,2,256]{2,1,0:T(2,128)(2,1)}, bf16[256,2,256]{2,1,0:T(2,128)(2,1)S(1)}, u32[]{:S(2)}, u32[]{:S(2)}) collective-permute-start(bf16[256,2,256]{2,1,0:T(2,128)(2,1)} %kv_hbm.1), channel_id=1, source_target_pairs={{0,2},{2,0},{4,6},{6,4},{8,10},{10,8},{12,14},{14,12},{16,18},{18,... | collective-permute-start | bytes 786440 | tf_op jit(solution)/shard_map/ppermute | solution.py:33
  2.0 10.8 %collective-permute-start.2 = (bf16[2,256,256]{2,1,0:T(8,128)(2,1)S(1)}, bf16[2,256,256]{2,1,0:T(8,128)(2,1)S(1)}, u32[]{:S(2)}, u32[]{:S(2)}) collective-permute-start(bf16[2,256,256]{2,1,0:T(8,128)(2,1)S(1)} %rotate.1.own), channel_id=1, source_target_pairs={{0,8},{4,12},{8,16},{12,20},{16,24},{20,28},{24,30},{28,26},{30,22... | collective-permute-start | bytes 786440 | tf_op jit(solution)/shard_map/ppermute | solution.py:28
  5.2 9.3 %collective-permute-start.1 = (bf16[2,256,256]{2,1,0:T(8,128)(2,1)S(1)}, bf16[2,256,256]{2,1,0:T(8,128)(2,1)S(1)}, u32[]{:S(2)}, u32[]{:S(2)}) collective-permute-start(bf16[2,256,256]{2,1,0:T(8,128)(2,1)S(1)} %rotate.1.own), channel_id=1, source_target_pairs={{0,4},{4,8},{8,12},{12,16},{16,20},{20,24},{24,28},{28,30},{30,26}... | collective-permute-start | bytes 786440 | tf_op jit(solution)/shard_map/ppermute | solution.py:28
  17.0 3.0 %collective-permute-start.4 = (bf16[2,2,256,256]{3,2,1,0:T(8,128)(2,1)S(1)}, bf16[2,2,256,256]{3,2,1,0:T(8,128)(2,1)S(1)}, u32[]{:S(2)}, u32[]{:S(2)}) collective-permute-start(bf16[2,2,256,256]{3,2,1,0:T(8,128)(2,1)S(1)} %pad_maximum_fusion.pair_ref), channel_id=1, source_target_pairs={{0,2},{2,0},{4,6},{6,4},{8,10},{10,8},{12,14},{14,12},{16,18},{18,... | collective-permute-start | bytes 1572872 | tf_op jit(solution)/shard_map/ppermute | solution.py:33
  18.0 11.1 %collective-permute-start.3 = (bf16[2,2,256,256]{3,2,1,0:T(8,128)(2,1)S(1)}, bf16[2,2,256,256]{3,2,1,0:T(8,128)(2,1)S(1)}, u32[]{:S(2)}, u32[]{:S(2)}) collective-permute-start(bf16[2,2,256,256]{3,2,1,0:T(8,128)(2,1)S(1)} %pad_maximum_fusion.pair_ref), channel_id=1, source_target_pairs={{0,8},{4,12},{8,16},{12,20},{16,24},{20,28},{24,30},{28,26},{30,22... | collective-permute-start | bytes 1572872 | tf_op jit(solution)/shard_map/ppermute | solution.py:28
  29.1 1.9 %collective-permute-start.5 = (bf16[2,2,256,256]{3,2,1,0:T(8,128)(2,1)S(1)}, bf16[2,2,256,256]{3,2,1,0:T(8,128)(2,1)S(1)}, u32[]{:S(2)}, u32[]{:S(2)}) collective-permute-start(bf16[2,2,256,256]{3,2,1,0:T(8,128)(2,1)S(1)} %collective-permute-done.3.pair_ref), channel_id=1, source_target_pairs={{0,2},{2,0},{4,6},{6,4},{8,10},{10,8},{12,14},{14,12},{16,18},{18,... | collective-permute-start | bytes 1572872 | tf_op jit(solution)/shard_map/ppermute | solution.py:33
